TPU v7x, 32 devices: a whole 2x2x4 slice. The times are simulated.
32 devices in a mesh: blk: 8 (over z, x), tile: 4 (over y, core).
Axes of the slice: x: 2, y: 2, z: 4, core: 2. Of those that a mesh axis runs over, the one named last changes fastest.
Arguments:
- stream_in: bfloat16 [32, 16, 16, 2240], P('tile', 'blk'), may hold values from -6 to 6
- queries: bfloat16 [32, 16, 16, 2240], P('tile', 'blk'), may hold values from -12 to 12
- key_rows: bfloat16 [32, 16, 16, 2240], P('tile', 'blk'), may hold values from -12 to 12
- value_rows: bfloat16 [32, 16, 16, 2240], P('tile', 'blk'), may hold values from -12 to 12
- w_output: bfloat16 [2240, 2240], P('tile'), may hold values from -0.125 to 0.125
- w_inner: bfloat16 [2240, 2, 4096], P(None, None, 'tile'), may hold values from -0.125 to 0.125
- w_down: bfloat16 [4096, 2240], P('tile'), may hold values from -0.09375 to 0.09375
- spatial_taps: float32 [3, 3, 2, 4096], P(None, None, None, 'tile'), may hold values from -2 to 2
- temporal_taps: float32 [3, 2, 4096], P(None, None, 'tile'), may hold values from -3.5 to 3.5
Outputs:
- layer_out: bfloat16 [32, 16, 16, 2240], P('tile', 'blk')
All inputs are finite; a program needn't handle non-finite values.
Results may differ from a plain program's by a relative error of at most 0.009.
Values may be sent and summed in bfloat16 or wider, within the bound.
A program may use at most 128 MiB of HBM per device.

v0:
```python
import functools

import jax
import jax.numpy as jnp
from jax import lax
from jax.experimental import pallas as pl
from jax.experimental.pallas import tpu as pltpu
from jax.sharding import PartitionSpec as P

HEADS = 20
HEAD_DIM = 112
TAPS = 3
BLOCK_F = 4
LANES = 128
EPS = 1e-06

MESH = pl.DeviceIdType.MESH


def vmem_specs(count):
    return [pl.BlockSpec(memory_space=pltpu.VMEM)] * count


def shifted(x, axis, by):
    peers = lax.axis_size(axis)
    pairs = [(i, i + by) for i in range(peers) if 0 <= i + by < peers]
    return lax.ppermute(x, axis, pairs)


def head_columns(head):
    return slice(head * HEAD_DIM, (head + 1) * HEAD_DIM)


def local_state_kernel(key_ref, value_ref, kv_ref):
    tokens = key_ref.shape[0]
    ones = jnp.ones((tokens, LANES - HEAD_DIM), jnp.bfloat16)
    for head in range(HEADS):
        keys = jnp.maximum(key_ref[:, head_columns(head)], 0)
        values = jnp.concatenate([value_ref[:, head_columns(head)], ones], axis=1)
        kv = lax.dot_general(
            keys, values, (((0,), (0,)), ((), ())), preferred_element_type=jnp.float32
        )
        kv_ref[head] = kv.astype(jnp.bfloat16)
    for head in range(HEADS, kv_ref.shape[0]):
        kv_ref[head] = jnp.zeros(kv_ref.shape[1:], jnp.bfloat16)


def exchange_kernel(
    blocks, pair, tiles, kv_ref, state_ref, got1, got2, total, block_send, final_send, states,
    send1, recv1, send2, recv2, send3, recv3,
):
    group = pair * tiles
    blk = lax.axis_index("blk")
    tile = lax.axis_index("tile")
    block = blk // pair
    member = blk % pair
    rank = member * tiles + tile

    def peer(step):
        other = (rank + step) % group
        return other, (block * pair + other // tiles, other % tiles)

    barrier = pltpu.get_barrier_semaphore()
    for step in range(1, group):
        pl.semaphore_signal(barrier, inc=1, device_id=peer(step)[1], device_id_type=MESH)
    for step in range(1, blocks):
        other = (block + step) % blocks
        pl.semaphore_signal(
            barrier, inc=1, device_id=(other * pair + member, tile), device_id_type=MESH
        )
    pl.semaphore_wait(barrier, group - 1 + blocks - 1)

    first = []
    for step in range(1, group):
        other, device = peer(step)
        copy = pltpu.make_async_remote_copy(
            src_ref=kv_ref.at[other], dst_ref=got1.at[step], send_sem=send1.at[step],
            recv_sem=recv1.at[step], device_id=device, device_id_type=MESH,
        )
        copy.start()
        first.append(copy)
    total[...] = kv_ref[rank].astype(jnp.float32)
    for step in range(1, group):
        first[step - 1].wait_recv()
        total[...] += got1[step].astype(jnp.float32)

    block_send[...] = total[...].astype(jnp.bfloat16)

    def later(step):
        return pltpu.make_async_remote_copy(
            src_ref=block_send, dst_ref=got2.at[step], send_sem=send2.at[step],
            recv_sem=recv2.at[step], device_id=(((block + step) % blocks) * pair + member, tile),
            device_id_type=MESH,
        )

    for step in range(1, blocks):

        @pl.when(block + step < blocks)
        def _():
            later(step).start()

    for step in range(1, blocks):

        @pl.when(block >= step)
        def _():
            later(step).wait_recv()
            total[...] += got2[step].astype(jnp.float32)

    final_send[...] = total[...].astype(jnp.bfloat16)
    third = []
    for step in range(1, group):
        copy = pltpu.make_async_remote_copy(
            src_ref=final_send, dst_ref=states.at[rank], send_sem=send3.at[step],
            recv_sem=recv3.at[step], device_id=peer(step)[1], device_id_type=MESH,
        )
        copy.start()
        third.append(copy)
    state_ref[rank] = total[...].astype(jnp.bfloat16)
    for step in range(1, group):
        third[step - 1].wait_recv()
        other = (rank + group - step) % group
        state_ref[other] = states[other]
    for step in range(1, group):
        first[step - 1].wait_send()
        third[step - 1].wait_send()
    for step in range(1, blocks):

        @pl.when(block + step < blocks)
        def _():
            later(step).wait_send()


def exchange_states(kv, blocks, pair, tiles):
    group = pair * tiles
    piece = kv.shape[1:]
    dma = pltpu.SemaphoreType.DMA
    return pl.pallas_call(
        functools.partial(exchange_kernel, blocks, pair, tiles),
        out_shape=jax.ShapeDtypeStruct(kv.shape, jnp.bfloat16),
        in_specs=vmem_specs(1),
        out_specs=vmem_specs(1)[0],
        scratch_shapes=[
            pltpu.VMEM((group,) + piece, jnp.bfloat16),
            pltpu.VMEM((blocks,) + piece, jnp.bfloat16),
            pltpu.VMEM(piece, jnp.float32),
            pltpu.VMEM(piece, jnp.bfloat16),
            pltpu.VMEM(piece, jnp.bfloat16),
            pltpu.VMEM((group,) + piece, jnp.bfloat16),
            dma((group,)),
            dma((group,)),
            dma((blocks,)),
            dma((blocks,)),
            dma((group,)),
            dma((group,)),
        ],
        compiler_params=pltpu.CompilerParams(collective_id=0, has_side_effects=True),
    )(kv)


def attention_kernel(query_ref, state_ref, out_ref):
    for head in range(HEADS):
        queries = jnp.maximum(query_ref[:, head_columns(head)], 0)
        both = jnp.dot(queries, state_ref[head], preferred_element_type=jnp.float32)
        ratio = both[:, :HEAD_DIM] / (both[:, HEAD_DIM : HEAD_DIM + 1] + EPS)
        out_ref[:, head_columns(head)] = ratio.astype(jnp.bfloat16)


def column_masks(stride, cols, width):
    col = lax.broadcasted_iota(jnp.int32, (stride, width), 0) % cols
    return col > 0, col < cols - 1


def fill_inner(hidden_ref, w_ref, inner, stride, chunk):
    tokens = hidden_ref.shape[0]
    edge = jnp.zeros((stride, inner.shape[1]), jnp.bfloat16)
    inner[:stride] = edge
    inner[stride + tokens :] = edge
    for start in range(0, tokens, chunk):
        product = jnp.dot(
            hidden_ref[start : start + chunk], w_ref[...], preferred_element_type=jnp.float32
        )
        inner[stride + start : stride + start + chunk] = jax.nn.silu(product).astype(jnp.bfloat16)


def conv_row(inner, taps_ref, row, stride, masks):
    rows = [
        inner[pl.ds(pl.multiple_of((row + a) * stride, stride), stride)].astype(jnp.float32)
        for a in range(3)
    ]
    sums = [
        sum(rows[a] * taps_ref[3 * a + b : 3 * a + b + 1] for a in range(3)) for b in range(3)
    ]
    from_left = jnp.where(masks[0], pltpu.roll(sums[0], 1, 0), 0.0)
    from_right = jnp.where(masks[1], pltpu.roll(sums[2], stride - 1, 0), 0.0)
    return sums[1] + from_left + from_right


def spatial_kernel(stride, cols, chunk, hidden_ref, w_ref, taps_ref, out_ref, inner):
    fill_inner(hidden_ref, w_ref, inner, stride, chunk)
    masks = column_masks(stride, cols, inner.shape[1])

    def body(row, carry):
        value = conv_row(inner, taps_ref, row, stride, masks)
        out_ref[pl.ds(pl.multiple_of(row * stride, stride), stride)] = value.astype(jnp.bfloat16)
        return carry

    lax.fori_loop(0, hidden_ref.shape[0] // stride, body, 0, unroll=2)


def gated_kernel(
    stride, cols, chunk, hidden_ref, wv_ref, wg_ref, sv_ref, sg_ref, tv_ref, tg_ref, ov_ref, og_ref,
    out_ref, inner_v, inner_g,
):
    fill_inner(hidden_ref, wv_ref, inner_v, stride, chunk)
    fill_inner(hidden_ref, wg_ref, inner_g, stride, chunk)
    masks = column_masks(stride, cols, inner_v.shape[1])

    def mixed(inner, taps_ref, time_ref, own_ref, row, where):
        before = conv_row(inner, taps_ref, row, stride, masks)
        before = before.astype(jnp.bfloat16).astype(jnp.float32)
        extended = jnp.concatenate([before, own_ref[where].astype(jnp.float32)], axis=0)
        total = extended[stride:] * time_ref[0:1]
        for lag in range(1, TAPS):
            start = stride - lag * cols
            total = total + extended[start : start + stride] * time_ref[lag : lag + 1]
        return total

    def body(row, carry):
        where = pl.ds(pl.multiple_of(row * stride, stride), stride)
        value = mixed(inner_v, sv_ref, tv_ref, ov_ref, row, where)
        gate = mixed(inner_g, sg_ref, tg_ref, og_ref, row, where)
        out_ref[where] = (value * jax.nn.silu(gate)).astype(jnp.bfloat16)
        return carry

    lax.fori_loop(0, hidden_ref.shape[0] // stride, body, 0)


def scatter_sum_kernel(
    rows, chunks, product_ref, hidden_ref, out_ref, got, sums, landed, send1, recv1, send2, recv2
):
    blk = lax.axis_index("blk")
    tile = lax.axis_index("tile")
    core = tile % 2
    y = tile // 2
    order = [step % rows for step in range(1, rows + 1)]

    barrier = pltpu.get_barrier_semaphore()
    pl.semaphore_signal(barrier, inc=1, device_id=(blk, y * 2 + 1 - core), device_id_type=MESH)
    for step in range(1, rows):
        pl.semaphore_signal(
            barrier, inc=1, device_id=(blk, ((y + step) % rows) * 2 + core), device_id_type=MESH
        )
    pl.semaphore_wait(barrier, rows)

    first = {}
    for step in order:
        there = (y + step) % rows
        for k in range(chunks):
            slot = step * chunks + k
            copy = pltpu.make_async_remote_copy(
                src_ref=product_ref.at[there * 2 + 1 - core, k], dst_ref=got.at[step, k],
                send_sem=send1.at[slot], recv_sem=recv1.at[slot],
                device_id=(blk, y * 2 + 1 - core), device_id_type=MESH,
            )
            copy.start()
            first[step, k] = copy
    second = {}
    for k in range(chunks):
        for step in range(1, rows):
            there = (y + step) % rows
            slot = step * chunks + k
            first[step, k].wait_recv()
            chip = product_ref[there * 2 + core, k].astype(jnp.float32) + got[step, k].astype(
                jnp.float32
            )
            sums[step, k] = chip.astype(jnp.bfloat16)
            copy = pltpu.make_async_remote_copy(
                src_ref=sums.at[step, k], dst_ref=landed.at[step, k],
                send_sem=send2.at[slot], recv_sem=recv2.at[slot],
                device_id=(blk, there * 2 + core), device_id_type=MESH,
            )
            copy.start()
            second[step, k] = copy
    for k in range(chunks):
        first[0, k].wait_recv()
        total = product_ref[tile, k].astype(jnp.float32) + got[0, k].astype(jnp.float32)
        for step in range(1, rows):
            second[step, k].wait_recv()
            total = total + landed[step, k].astype(jnp.float32)
        out_ref[k] = (hidden_ref[k].astype(jnp.float32) + total).astype(jnp.bfloat16)
    for copy in list(first.values()) + list(second.values()):
        copy.wait_send()


def scatter_sum(product, hidden, tiles):
    rows = tiles // 2
    chunks = 4
    tokens, width = hidden.shape
    piece = (chunks, tokens // chunks, width)
    bf16 = jnp.bfloat16
    sems = [pltpu.SemaphoreType.DMA((rows * chunks,))] * 4
    return pl.pallas_call(
        functools.partial(scatter_sum_kernel, rows, chunks),
        out_shape=jax.ShapeDtypeStruct(piece, bf16),
        in_specs=vmem_specs(2),
        out_specs=vmem_specs(1)[0],
        scratch_shapes=[pltpu.VMEM((rows,) + piece, bf16)] * 3 + sems,
        compiler_params=pltpu.CompilerParams(
            collective_id=1, has_side_effects=True, vmem_limit_bytes=40 * 2**20
        ),
    )(product.reshape((tiles,) + piece), hidden.reshape(piece))


def project_kernel(x_ref, w_ref, out_ref):
    product = jnp.dot(x_ref[...], w_ref[...], preferred_element_type=jnp.float32)
    out_ref[...] = product.astype(jnp.bfloat16)


def on_device(
    stream_in, queries, key_rows, value_rows, w_output, w_inner, w_down, spatial_taps, temporal_taps
):
    row_count, frames, col_count, width = queries.shape
    tokens = row_count * frames * col_count
    tiles = lax.axis_size("tile")
    pair = BLOCK_F // frames
    blocks = lax.axis_size("blk") // pair
    group = pair * tiles
    per_rank = -(-HEADS // group)
    bf16 = jnp.bfloat16

    w_full = lax.all_gather(w_output, "tile", axis=0, tiled=True)

    kv = pl.pallas_call(
        local_state_kernel,
        out_shape=jax.ShapeDtypeStruct((group * per_rank, HEAD_DIM, LANES), bf16),
        in_specs=vmem_specs(2),
        out_specs=vmem_specs(1)[0],
    )(key_rows.reshape(tokens, width), value_rows.reshape(tokens, width))
    state = exchange_states(
        kv.reshape(group, per_rank, HEAD_DIM, LANES), blocks, pair, tiles
    ).reshape(group * per_rank, HEAD_DIM, LANES)
    attended = pl.pallas_call(
        attention_kernel,
        out_shape=jax.ShapeDtypeStruct((tokens, width), bf16),
        in_specs=vmem_specs(2),
        out_specs=vmem_specs(1)[0],
    )(queries.reshape(tokens, width), state)

    attn_out = jnp.dot(attended, w_full, preferred_element_type=jnp.float32)
    hidden = (stream_in.reshape(tokens, width).astype(jnp.float32) + attn_out).astype(bf16)

    chan = w_inner.shape[2]
    w_flat = w_inner.reshape(width, 2 * chan)
    space = spatial_taps.reshape(9, 2 * chan)
    time = temporal_taps.reshape(TAPS, 2 * chan)
    before = shifted(hidden, "blk", 1)
    own_all = lax.all_gather(hidden, "tile", axis=0, tiled=True)
    before_all = lax.all_gather(before, "tile", axis=0, tiled=True)

    whole = tokens * tiles
    stride = frames * col_count
    lane_block = 256
    chunk = 256
    value_blocks = chan // lane_block
    full = lambda rows: pl.BlockSpec((rows, width), lambda j: (0, 0))
    block = lambda rows: pl.BlockSpec((rows, lane_block), lambda j: (0, j))
    gate = lambda rows: pl.BlockSpec((rows, lane_block), lambda j: (0, j + value_blocks))
    inner_scratch = pltpu.VMEM((whole + 2 * stride, lane_block), bf16)
    flops = 2 * whole * width * 2 * chan
    cost = pl.CostEstimate(
        flops=flops, bytes_accessed=2 * (whole * width + 2 * width * chan), transcendentals=0
    )
    spatial = pl.pallas_call(
        functools.partial(spatial_kernel, stride, col_count, chunk),
        grid=(2 * value_blocks,),
        out_shape=jax.ShapeDtypeStruct((whole, 2 * chan), bf16),
        in_specs=[full(whole), block(width), block(9)],
        out_specs=block(whole),
        scratch_shapes=[inner_scratch],
        cost_estimate=cost,
        compiler_params=pltpu.CompilerParams(vmem_limit_bytes=40 * 2**20),
    )(own_all, w_flat, space)
    gated_out = pl.pallas_call(
        functools.partial(gated_kernel, stride, col_count, chunk),
        grid=(value_blocks,),
        out_shape=jax.ShapeDtypeStruct((whole, chan), bf16),
        in_specs=[
            full(whole), block(width), gate(width), block(9), gate(9), block(TAPS), gate(TAPS),
            block(whole), gate(whole),
        ],
        out_specs=block(whole),
        scratch_shapes=[inner_scratch, inner_scratch],
        cost_estimate=cost,
        compiler_params=pltpu.CompilerParams(vmem_limit_bytes=48 * 2**20),
    )(before_all, w_flat, w_flat, space, space, time, time, spatial, spatial)

    product = pl.pallas_call(
        project_kernel,
        grid=(whole // chunk,),
        out_shape=jax.ShapeDtypeStruct((whole, width), bf16),
        in_specs=[
            pl.BlockSpec((chunk, chan), lambda j: (j, 0)),
            pl.BlockSpec((chan, width), lambda j: (0, 0)),
        ],
        out_specs=pl.BlockSpec((chunk, width), lambda j: (j, 0)),
        compiler_params=pltpu.CompilerParams(vmem_limit_bytes=32 * 2**20),
    )(gated_out, w_down)
    layer_out = scatter_sum(product, hidden, tiles)
    return layer_out.reshape(queries.shape)


def solution(mesh):
    in_specs = (
        P("tile", "blk", None, None),
        P("tile", "blk", None, None),
        P("tile", "blk", None, None),
        P("tile", "blk", None, None),
        P("tile", None),
        P(None, None, "tile"),
        P("tile", None),
        P(None, None, None, "tile"),
        P(None, None, "tile"),
    )
    out_specs = P("tile", "blk", None, None)
    return jax.shard_map(
        on_device, mesh=mesh, in_specs=in_specs, out_specs=out_specs, check_vma=False
    )
```

profile of v0, /device:TPU:9, one launch (start us, length us, event | category | flops | bytes accessed | tf_op | source)
XLA Modules:
  0.0 243.5 jit_solution(8555530427074140557)
XLA Ops:
  6.5 0.7 all-gather.4.cloned.1.call-update
  7.3 0.0 all-gather.8.cloned.1.call-start
  7.3 4.9 %shard_map.91 = bf16[24,112,128]{2,1,0:T(8,128)(2,1)} custom-call(bf16[256,2240]{1,0:T(8,128)(2,1)} %bitcast.34, bf16[256,2240]{1,0:T(8,128)(2,1)} %bitcast.35), custom_call_target="tpu_custom_call" | custom-call | tf_op jit(solution)/shard_map/pallas_call | solution.py:333
  12.2 34.4 %shard_map.92 = bf16[8,3,112,128]{3,2,1,0:T(8,128)(2,1)} custom-call(bf16[8,3,112,128]{3,2,1,0:T(8,128)(2,1)} %bitcast.33), custom_call_target="tpu_custom_call" | custom-call | tf_op jit(solution)/shard_map/pallas_call | solution.py:137
  46.6 7.1 %shard_map.93 = bf16[256,2240]{1,0:T(8,128)(2,1)} custom-call(bf16[256,2240]{1,0:T(8,128)(2,1)} %bitcast.36, bf16[24,112,128]{2,1,0:T(8,128)(2,1)} %bitcast.32), custom_call_target="tpu_custom_call" | custom-call | tf_op jit(solution)/shard_map/pallas_call | solution.py:342
  53.8 36.5 %all-gather.4.cloned.1.call-done = bf16[2240,2240]{1,0:T(8,128)(2,1)} async-done(((bf16[560,2240]{1,0:T(8,128)(2,1)}), bf16[2240,2240]{1,0:T(8,128)(2,1)}) %all-gather.4.cloned.1.call-update) | async-done | bytes 10035216 | tf_op jit(solution)/shard_map/all_gather | solution.py:331
  90.3 8.2 %fusion = bf16[256,2240]{1,0:T(8,128)(2,1)} fusion(bf16[256,2240]{1,0:T(8,128)(2,1)} %shard_map.93, bf16[2240,2240]{1,0:T(8,128)(2,1)} %all-gather.4.cloned.1.call-done, bf16[256,2240]{1,0:T(8,128)(2,1)S(1)} %bitcast.40), kind=kOutput, calls=%fused_computation.1 | convolution fusion | flops 2570731520 | bytes 13475840 | tf_op jit(solution)/shard_map/dot_general | solution.py:349
  98.5 0.0 all-gather.8.cloned.1.call-update
  98.5 0.0 all-gather.6.cloned.1.call-start
  98.6 1.7 copy.13
  100.3 3.3 %collective-permute-start = (bf16[256,2240]{0,1:T(8,128)(2,1)S(1)}, bf16[256,2240]{0,1:T(8,128)(2,1)S(1)}, u32[]{:S(2)}, u32[]{:S(2)}) collective-permute-start(bf16[256,2240]{0,1:T(8,128)(2,1)S(1)} %copy.13), channel_id=1, source_target_pairs={{0,4},{4,8},{8,12},{12,16},{16,20},{20,24},{24,28},{1,5},{5,9},{9,... | collective-permute-start | bytes 3440648 | tf_op jit(solution)/shard_map/ppermute | solution.py:27
  103.6 26.1 %collective-permute-done = bf16[256,2240]{0,1:T(8,128)(2,1)S(1)} collective-permute-done((bf16[256,2240]{0,1:T(8,128)(2,1)S(1)}, bf16[256,2240]{0,1:T(8,128)(2,1)S(1)}, u32[]{:S(2)}, u32[]{:S(2)}) %collective-permute-start) | collective-permute-done | bytes 1146912 | tf_op jit(solution)/shard_map/ppermute | solution.py:27
  129.6 1.5 copy.14
  131.2 0.0 all-gather.6.cloned.1.call-update
  131.2 11.1 %copy.17 = bf16[280,8,2,1024]{3,1,2,0:T(8,128)(2,1)} copy(bf16[280,8,2,1024]{3,2,1,0:T(2,128)(2,1)} %bitcast.28) | data formatting | bytes 18350080
  142.4 7.0 %copy.15.w_ref = bf16[1024,2240]{1,0:T(8,128)(2,1)} copy(bf16[1024,2240]{0,1:T(8,128)(2,1)} %param.15) | data formatting | bytes 9175040 | tf_op args[6]
  149.5 2.3 copy-done.2
  151.8 21.2 %shard_map.94.ov_ref.og_ref = bf16[1024,2048]{1,0:T(8,128)(2,1)S(1)} custom-call(bf16[1024,2240]{1,0:T(8,128)(2,1)S(1)} %copy-done.2, bf16[2240,2048]{1,0:T(8,128)(2,1)} %bitcast.29, f32[9,2048]{1,0:T(8,128)S(1)} %bitcast.23), custom_call_target="tpu_custom_call" | custom-call | flops 9395240960 | bytes 13762560 | tf_op jit(solution)/shard_map/pallas_call | solution.py:373
  173.0 2.0 copy-done.3
  175.0 0.3 all-gather.6.cloned.1.call-done.hidden_ref
  175.4 24.9 %shard_map.95.x_ref = bf16[1024,1024]{1,0:T(8,128)(2,1)S(1)} custom-call(bf16[1024,2240]{1,0:T(8,128)(2,1)} %all-gather.6.cloned.1.call-done.hidden_ref, bf16[2240,2048]{1,0:T(8,128)(2,1)} %bitcast.30, bf16[2240,2048]{1,0:T(8,128)(2,1)} %bitcast.31, f32[9,2048]{1,0:T(8,128)S(1)} %bitcast.24, f32[9,2048]{1,0:T(8,128)S(1)} %bitcast.25, ...), custom_call_target="tpu_custom_call" | custom-call | flops 9395240960 | bytes 13762560 | tf_op jit(solution)/shard_map/pallas_call | solution.py:383
  200.3 5.6 %shard_map.96 = bf16[1024,2240]{1,0:T(8,128)(2,1)S(1)} custom-call(bf16[1024,1024]{1,0:T(8,128)(2,1)S(1)} %shard_map.95.x_ref, bf16[1024,2240]{1,0:T(8,128)(2,1)S(1)} %copy-done), custom_call_target="tpu_custom_call" | custom-call | tf_op jit(solution)/shard_map/pallas_call | solution.py:397
  205.9 30.0 %shard_map.97 = bf16[4,64,2240]{2,1,0:T(8,128)(2,1)S(1)} custom-call(bf16[4,4,64,2240]{3,2,1,0:T(8,128)(2,1)S(1)} %bitcast.20, bf16[4,64,2240]{2,1,0:T(8,128)(2,1)S(1)} %bitcast.21), custom_call_target="tpu_custom_call" | custom-call | tf_op jit(solution)/shard_map/pallas_call | solution.py:302
  235.9 1.0 copy.21
  (17 shorter events, 0.1 us)
Async XLA Ops:
  6.5 83.7 %all-gather.4.cloned.1.call-start = ((), (), s32[]{:S(2)}) async-start(), calls=%async_computation | async-start | bytes 12902400 | tf_op jit(solution)/shard_map/all_gather | solution.py:331
  7.3 142.2 %all-gather.8.cloned.1.call-start = ((), (), s32[]{:S(2)}) async-start(), calls=%async_computation.2 | async-start | bytes 5898240 | tf_op jit(solution)/shard_map/all_gather | solution.py:357
  12.2 78.1 %copy-start.6 = (bf16[8,2,16,2240]{3,2,1,0:T(8,128)(2,1)S(1)}, bf16[8,2,16,2240]{3,2,1,0:T(8,128)(2,1)}, u32[]{:S(2)}) copy-start(bf16[8,2,16,2240]{3,2,1,0:T(8,128)(2,1)} %param.9) | copy-start | bytes 3440644
  98.5 76.9 %all-gather.6.cloned.1.call-start = ((), (), s32[]{:S(2)}) async-start(), calls=%async_computation.1 | async-start | bytes 5898240 | tf_op jit(solution)/shard_map/all_gather | solution.py:358
  100.3 29.4 %collective-permute-start = (bf16[256,2240]{0,1:T(8,128)(2,1)S(1)}, bf16[256,2240]{0,1:T(8,128)(2,1)S(1)}, u32[]{:S(2)}, u32[]{:S(2)}) collective-permute-start(bf16[256,2240]{0,1:T(8,128)(2,1)S(1)} %copy.13), channel_id=1, source_target_pairs={{0,4},{4,8},{8,12},{12,16},{16,20},{20,24},{24,28},{1,5},{5,9},{9,... | collective-permute-start | bytes 3440648 | tf_op jit(solution)/shard_map/ppermute | solution.py:27
  131.2 11.1 %copy-start.4 = (f32[3,3,2,1024]{3,2,1,0:T(2,128)S(1)}, f32[3,3,2,1024]{3,2,1,0:T(2,128)}, u32[]{:S(2)}) copy-start(f32[3,3,2,1024]{3,2,1,0:T(2,128)} %param.16) | copy-start | bytes 221188
  131.2 11.2 %copy-start.5 = (f32[3,2,1024]{2,1,0:T(2,128)S(1)}, f32[3,2,1024]{2,1,0:T(2,128)}, u32[]{:S(2)}) copy-start(f32[3,2,1024]{2,1,0:T(2,128)} %param.17) | copy-start | bytes 73732
  149.5 2.3 copy-start.2
  173.0 2.0 copy-start.3
  175.4 24.9 %copy-start = (bf16[1024,2240]{1,0:T(8,128)(2,1)S(1)}, bf16[1024,2240]{1,0:T(8,128)(2,1)}, u32[]{:S(2)}) copy-start(bf16[1024,2240]{1,0:T(8,128)(2,1)} %copy.15.w_ref) | copy-start | bytes 13762564
  200.3 5.6 %copy-start.1 = (bf16[256,2240]{1,0:T(8,128)(2,1)S(1)}, bf16[256,2240]{1,0:T(8,128)(2,1)}, u32[]{:S(2)}) copy-start(bf16[256,2240]{1,0:T(8,128)(2,1)} %fusion) | copy-start | bytes 3440644
Sparse Core Ops, SparseCore 0:
  8.9 81.3 all-gather.3
  98.7 37.6 all-gather.7
  137.9 37.4 all-gather.5
where the time goes:
time: 245 us; the launch traced here: 243 us
  Pallas kernels  128 us (52%)
  waiting for transfers between devices  63.7 us (26%)
  local copies, waits for them, and re-layouts  26.8 us (11%)
  between operations  13.2 us (5%)
  matrix products  8.23 us (3%)
  starting transfers between devices  3.36 us (1%)
    all_gather x1, waiting for transfers between devices, on_device(): w_full = lax.all_gather(w_output, 'tile', axis=0, tiled=True)  36.5 us
    pallas_call x1, Pallas kernels, exchange_states(): pl.pallas_call(functools.partial(exchange_kernel, blocks, pair, tiles), o...  34.4 us
    pallas_call x1, Pallas kernels, scatter_sum(): pl.pallas_call(functools.partial(scatter_sum_kernel, rows, chunks), out_s...  30 us
    ppermute x1, waiting for transfers between devices, shifted(): return lax.ppermute(x, axis, pairs)  26.1 us
    pallas_call x1, Pallas kernels, on_device(): pl.pallas_call(functools.partial(gated_kernel, stride, col_count, chunk),...  24.9 us
    unnamed x20, local copies, waits for them, and re-layouts  23.6 us
    pallas_call x1, Pallas kernels, on_device(): pl.pallas_call(functools.partial(spatial_kernel, stride, col_count, chunk...  21.2 us
    dot_general x1, matrix products, on_device(): attn_out = jnp.dot(attended, w_full, preferred_element_type=jnp.float32)  8.23 us
  transfers between devices with their start and end apart: 4, of which 3 were waited for; matrix products, arithmetic and copies ran while one was open for 9% of the time, Pallas kernels for 28%

commit v1 on v0

--- a/solution.py
+++ b/solution.py
@@ -21,76 +21,163 @@
     return [pl.BlockSpec(memory_space=pltpu.VMEM)] * count
 
 
-def shifted(x, axis, by):
-    peers = lax.axis_size(axis)
-    pairs = [(i, i + by) for i in range(peers) if 0 <= i + by < peers]
-    return lax.ppermute(x, axis, pairs)
-
-
 def head_columns(head):
     return slice(head * HEAD_DIM, (head + 1) * HEAD_DIM)
 
 
-def local_state_kernel(key_ref, value_ref, kv_ref):
-    tokens = key_ref.shape[0]
+def rows_of(i, parts, rows):
+    units = -(-rows // 16)
+    low, high = i * units // parts, (i + 1) * units // parts
+    return slice(low * 16, min(high * 16, rows))
+
+
+def front_kernel(
+    dims, query_ref, key_ref, value_ref, stream_ref, w_ref, inner_ref, hidden_ref, flat_ref,
+    wbuf, raw, flat, kv, got0, csum, got1, got2, total, block_send, final_send, state,
+    attended, pieces, acc, local, core_s, core_r, ysend, yrecv, xsend, xrecv, csend, crecv,
+    send1, recv1, send2, recv2, send3, recv3, send4, recv4,
+):
+    blocks, pair, ways, subs = dims
+    rows = w_ref.shape[0]
+    tokens, width = hidden_ref.shape
+    chan = inner_ref.shape[2]
+    group = pair * ways
+    per_core = -(-HEADS // 2)
+    per_rank = kv.shape[2]
+    blk = lax.axis_index("blk")
+    tile = lax.axis_index("tile")
+    core = tile % 2
+    y = tile // 2
+    block = blk // pair
+    member = blk % pair
+    rank = member * ways + y
+    sibling = (blk, y * 2 + 1 - core)
+    ids = pair * subs
+
+    def remote(src, dst, send, recv, device):
+        return pltpu.make_async_remote_copy(
+            src_ref=src, dst_ref=dst, send_sem=send, recv_sem=recv, device_id=device,
+            device_id_type=MESH,
+        )
+
+    raw_copy = pltpu.make_async_copy(inner_ref, raw, local.at[0])
+    own_copy = pltpu.make_async_copy(w_ref, wbuf.at[tile], local.at[1])
+    raw_copy.start()
+    own_copy.start()
+
+    def peer(step):
+        other = (rank + step) % group
+        return other, (block * pair + other // ways, (other % ways) * 2 + core)
+
+    def other_block(step):
+        return (((block + step) % blocks) * pair + member, tile)
+
+    barrier = pltpu.get_barrier_semaphore()
+    pl.semaphore_signal(barrier, inc=1, device_id=sibling, device_id_type=MESH)
+    for step in range(1, group):
+        pl.semaphore_signal(barrier, inc=1, device_id=peer(step)[1], device_id_type=MESH)
+    for step in range(1, blocks):
+        pl.semaphore_signal(barrier, inc=1, device_id=other_block(step), device_id_type=MESH)
+    pl.semaphore_wait(barrier, group + blocks - 1)
+
+    w_core = remote(w_ref, wbuf.at[tile], core_s.at[0], core_r.at[0], sibling)
+    w_core.start()
+
+    def y_send(s, j, i):
+        part = rows_of(i * subs + j, ids, rows)
+        return remote(
+            w_ref.at[part], wbuf.at[tile, part], ysend.at[s, j], yrecv.at[s, j],
+            (blk, ((y + s) % ways) * 2 + core),
+        )
+
+    def came(s):
+        return ((y + ways - s) % ways) * 2 + core
+
+    def x_send(s, j, st, i):
+        part = rows_of(i * subs + j, ids, rows)
+        place = wbuf.at[came(s), part]
+        return remote(
+            place, place, xsend.at[st, s, j], xrecv.at[st, s, j],
+            (block * pair + (member + st) % pair, tile),
+        )
+
+    def core_send(s, number):
+        part = rows_of(number, ids, rows)
+        place = wbuf.at[came(s), part]
+        return remote(place, place, csend.at[s, number], crecv.at[s, number], sibling)
+
+    def each_member(body):
+        for i in range(pair):
+            pl.when(member == i)(functools.partial(body, i))
+
+    def start_y(j):
+        def body(i):
+            for s in range(1, ways):
+                y_send(s, j, i).start()
+
+        each_member(body)
+
+    def relay_y(j):
+        def body(i):
+            for s in range(1, ways):
+                y_send(s, j, i).wait_recv()
+                for st in range(1, pair):
+                    x_send(s, j, st, i).start()
+                core_send(s, i * subs + j).start()
+
+        each_member(body)
+
+    def relay_x(j):
+        def body(i):
+            for s in range(1, ways):
+                for st in range(1, pair):
+                    source = (i + pair - st) % pair
+                    x_send(s, j, st, source).wait_recv()
+                    core_send(s, source * subs + j).start()
+
+        each_member(body)
+
+    start_y(0)
+
     ones = jnp.ones((tokens, LANES - HEAD_DIM), jnp.bfloat16)
+    slots = group * per_rank
     for head in range(HEADS):
         keys = jnp.maximum(key_ref[:, head_columns(head)], 0)
         values = jnp.concatenate([value_ref[:, head_columns(head)], ones], axis=1)
-        kv = lax.dot_general(
+        product = lax.dot_general(
             keys, values, (((0,), (0,)), ((), ())), preferred_element_type=jnp.float32
         )
-        kv_ref[head] = kv.astype(jnp.bfloat16)
-    for head in range(HEADS, kv_ref.shape[0]):
-        kv_ref[head] = jnp.zeros(kv_ref.shape[1:], jnp.bfloat16)
-
-
-def exchange_kernel(
-    blocks, pair, tiles, kv_ref, state_ref, got1, got2, total, block_send, final_send, states,
-    send1, recv1, send2, recv2, send3, recv3,
-):
-    group = pair * tiles
-    blk = lax.axis_index("blk")
-    tile = lax.axis_index("tile")
-    block = blk // pair
-    member = blk % pair
-    rank = member * tiles + tile
-
-    def peer(step):
-        other = (rank + step) % group
-        return other, (block * pair + other // tiles, other % tiles)
-
-    barrier = pltpu.get_barrier_semaphore()
-    for step in range(1, group):
-        pl.semaphore_signal(barrier, inc=1, device_id=peer(step)[1], device_id_type=MESH)
-    for step in range(1, blocks):
-        other = (block + step) % blocks
-        pl.semaphore_signal(
-            barrier, inc=1, device_id=(other * pair + member, tile), device_id_type=MESH
-        )
-    pl.semaphore_wait(barrier, group - 1 + blocks - 1)
-
+        half, i = head // per_core, head % per_core
+        kv[half, i // per_rank, i % per_rank] = product.astype(jnp.bfloat16)
+    for half in range(2):
+        for i in range(slots):
+            if i >= per_core or half * per_core + i >= HEADS:
+                kv[half, i // per_rank, i % per_rank] = jnp.zeros(kv.shape[3:], jnp.bfloat16)
+
+    kv_core = remote(kv.at[1 - core], got0, core_s.at[1], core_r.at[1], sibling)
+    kv_core.start()
+    relay_y(0)
+    kv_core.wait_recv()
+    for r in range(group):
+        csum[r] = (kv[core, r].astype(jnp.float32) + got0[r].astype(jnp.float32)).astype(
+            jnp.bfloat16
+        )
     first = []
     for step in range(1, group):
         other, device = peer(step)
-        copy = pltpu.make_async_remote_copy(
-            src_ref=kv_ref.at[other], dst_ref=got1.at[step], send_sem=send1.at[step],
-            recv_sem=recv1.at[step], device_id=device, device_id_type=MESH,
-        )
+        copy = remote(csum.at[other], got1.at[step], send1.at[step], recv1.at[step], device)
         copy.start()
         first.append(copy)
-    total[...] = kv_ref[rank].astype(jnp.float32)
+    start_y(1)
+    total[...] = kv[core, rank].astype(jnp.float32) + got0[rank].astype(jnp.float32)
     for step in range(1, group):
         first[step - 1].wait_recv()
         total[...] += got1[step].astype(jnp.float32)
-
     block_send[...] = total[...].astype(jnp.bfloat16)
 
     def later(step):
-        return pltpu.make_async_remote_copy(
-            src_ref=block_send, dst_ref=got2.at[step], send_sem=send2.at[step],
-            recv_sem=recv2.at[step], device_id=(((block + step) % blocks) * pair + member, tile),
-            device_id_type=MESH,
+        return remote(
+            block_send, got2.at[step], send2.at[step], recv2.at[step], other_block(step)
         )
 
     for step in range(1, blocks):
@@ -98,6 +185,27 @@
         @pl.when(block + step < blocks)
         def _():
             later(step).start()
+
+    raw_copy.wait()
+
+    def deinterleave(start, count):
+        def body(n, carry):
+            where = pl.ds(pl.multiple_of(n * 64, 64), 64)
+            both = raw[where]
+            flat[where, 0:chan] = both[:, 0, :]
+            flat[where, chan : 2 * chan] = both[:, 1, :]
+            return carry
+
+        lax.fori_loop(start, start + count, body, 0)
+
+    steps = width // 64
+    deinterleave(0, steps // 2)
+    relay_y(1)
+    start_y(2)
+    relay_x(0)
+    deinterleave(steps // 2, steps - steps // 2)
+    flat_copy = pltpu.make_async_copy(flat, flat_ref, local.at[2])
+    flat_copy.start()
 
     for step in range(1, blocks):
 
@@ -109,60 +217,300 @@
     final_send[...] = total[...].astype(jnp.bfloat16)
     third = []
     for step in range(1, group):
-        copy = pltpu.make_async_remote_copy(
-            src_ref=final_send, dst_ref=states.at[rank], send_sem=send3.at[step],
-            recv_sem=recv3.at[step], device_id=peer(step)[1], device_id_type=MESH,
+        copy = remote(
+            final_send, state.at[core, rank], send3.at[step], recv3.at[step], peer(step)[1]
         )
         copy.start()
         third.append(copy)
-    state_ref[rank] = total[...].astype(jnp.bfloat16)
+    fourth = [remote(final_send, state.at[core, rank], send4.at[0], recv4.at[0], sibling)]
+    fourth[0].start()
+    state[core, rank] = total[...].astype(jnp.bfloat16)
+    relay_y(2)
+    start_y(3)
+    relay_x(1)
     for step in range(1, group):
         third[step - 1].wait_recv()
-        other = (rank + group - step) % group
-        state_ref[other] = states[other]
-    for step in range(1, group):
-        first[step - 1].wait_send()
-        third[step - 1].wait_send()
+        place = state.at[core, (rank + group - step) % group]
+        copy = remote(place, place, send4.at[step], recv4.at[step], sibling)
+        copy.start()
+        fourth.append(copy)
+    for copy in fourth:
+        copy.wait_recv()
+
+    for head in range(HEADS):
+        half, i = head // per_core, head % per_core
+        queries = jnp.maximum(query_ref[:, head_columns(head)], 0)
+        both = jnp.dot(
+            queries, state[half, i // per_rank, i % per_rank], preferred_element_type=jnp.float32
+        )
+        ratio = both[:, :HEAD_DIM] / (both[:, HEAD_DIM : HEAD_DIM + 1] + EPS)
+        attended[:, head_columns(head)] = ratio.astype(jnp.bfloat16)
+    relay_y(3)
+    relay_x(2)
+    for t in range(2 * ways):
+        pieces[t] = attended[:, t * rows : (t + 1) * rows]
+
+    acc[...] = stream_ref[...].astype(jnp.float32)
+
+    def add_piece(step, carry):
+        t = ((y + step // 2) % ways) * 2 + (core + step) % 2
+        acc[...] += jnp.dot(pieces[t], wbuf[t], preferred_element_type=jnp.float32)
+        return carry
+
+    own_copy.wait()
+    w_core.wait_recv()
+    lax.fori_loop(0, 2, add_piece, 0)
+    relay_x(3)
+    for s in range(1, ways):
+        for number in range(ids):
+            core_send(s, number).wait_recv()
+    lax.fori_loop(2, 2 * ways, add_piece, 0)
+    hidden_ref[...] = acc[...].astype(jnp.bfloat16)
+
+    flat_copy.wait()
+    w_core.wait_send()
+    kv_core.wait_send()
+    for copy in first + third + fourth:
+        copy.wait_send()
     for step in range(1, blocks):
 
         @pl.when(block + step < blocks)
         def _():
             later(step).wait_send()
 
-
-def exchange_states(kv, blocks, pair, tiles):
-    group = pair * tiles
-    piece = kv.shape[1:]
+    def sent(i):
+        for s in range(1, ways):
+            for j in range(subs):
+                y_send(s, j, i).wait_send()
+                for st in range(1, pair):
+                    x_send(s, j, st, i).wait_send()
+
+    each_member(sent)
+    for s in range(1, ways):
+        for number in range(ids):
+            core_send(s, number).wait_send()
+
+
+def front(query, key, value, stream, w_output, w_inner, blocks, pair, tiles):
+    ways, subs = tiles // 2, 4
+    group = pair * ways
+    per_rank = -(-(-(-HEADS // 2)) // group)
+    tokens, width = query.shape
+    rows = w_output.shape[0]
+    chan = w_inner.shape[2]
+    bf16, f32 = jnp.bfloat16, jnp.float32
+    dma = pltpu.SemaphoreType.DMA
+    piece = (per_rank, HEAD_DIM, LANES)
+    vmem = pltpu.VMEM
+    anywhere = pl.BlockSpec(memory_space=pl.ANY)
+    inside = pl.BlockSpec(memory_space=pltpu.VMEM)
+    return pl.pallas_call(
+        functools.partial(front_kernel, (blocks, pair, ways, subs)),
+        out_shape=[
+            jax.ShapeDtypeStruct((tokens, width), bf16),
+            jax.ShapeDtypeStruct((width, 2 * chan), bf16),
+        ],
+        in_specs=[inside] * 4 + [anywhere] * 2,
+        out_specs=[inside, anywhere],
+        scratch_shapes=[
+            vmem((tiles, rows, width), bf16),
+            vmem(w_inner.shape, bf16),
+            vmem((width, 2 * chan), bf16),
+            vmem((2, group) + piece, bf16),
+            vmem((group,) + piece, bf16),
+            vmem((group,) + piece, bf16),
+            vmem((group,) + piece, bf16),
+            vmem((blocks,) + piece, bf16),
+            vmem(piece, f32),
+            vmem(piece, bf16),
+            vmem(piece, bf16),
+            vmem((2, group) + piece, bf16),
+            vmem((tokens, width), bf16),
+            vmem((tiles, tokens, rows), bf16),
+            vmem((tokens, width), f32),
+            dma((3,)),
+            dma((2,)),
+            dma((2,)),
+            dma((ways, subs)),
+            dma((ways, subs)),
+            dma((pair, ways, subs)),
+            dma((pair, ways, subs)),
+            dma((ways, pair * subs)),
+            dma((ways, pair * subs)),
+        ]
+        + [dma((group,))] * 2
+        + [dma((blocks,))] * 2
+        + [dma((group,))] * 4,
+        compiler_params=pltpu.CompilerParams(
+            collective_id=0, has_side_effects=True, vmem_limit_bytes=60 * 2**20
+        ),
+    )(query, key, value, stream, w_output, w_inner)
+
+
+def spread_kernel(
+    dims, hidden_ref, own_ref, before_ref, local, core_s, core_r, ysend, yrecv, bsend, brecv,
+):
+    ways, halves, blks = dims
+    tokens = hidden_ref.shape[0]
+    part = tokens // halves
+    blk = lax.axis_index("blk")
+    tile = lax.axis_index("tile")
+    core = tile % 2
+    y = tile // 2
+    sibling = (blk, y * 2 + 1 - core)
+    follower = ((blk + 1) % blks, tile)
+
+    def remote(src, dst, send, recv, device):
+        return pltpu.make_async_remote_copy(
+            src_ref=src, dst_ref=dst, send_sem=send, recv_sem=recv, device_id=device,
+            device_id_type=MESH,
+        )
+
+    def other(s):
+        return (blk, ((y + s) % ways) * 2 + core)
+
+    def came(s):
+        return ((y + ways - s) % ways) * 2 + core
+
+    barrier = pltpu.get_barrier_semaphore()
+    pl.semaphore_signal(barrier, inc=1, device_id=sibling, device_id_type=MESH)
+    for s in range(1, ways):
+        pl.semaphore_signal(barrier, inc=1, device_id=other(s), device_id_type=MESH)
+    pl.semaphore_signal(barrier, inc=1, device_id=follower, device_id_type=MESH)
+    pl.semaphore_signal(
+        barrier, inc=1, device_id=((blk + blks - 1) % blks, tile), device_id_type=MESH
+    )
+    pl.semaphore_wait(barrier, ways + 2)
+
+    def rows_at(t, h):
+        return pl.ds(pl.multiple_of(t * tokens + h * part, part), part)
+
+    def piece(ref, t, h):
+        return ref.at[rows_at(t, h)]
+
+    def source(h):
+        return hidden_ref.at[pl.ds(h * part, part)]
+
+    def own_core(h):
+        return remote(source(h), piece(own_ref, tile, h), core_s.at[0, 0, h], core_r.at[0, 0, h], sibling)
+
+    def own_y(s, h):
+        return remote(source(h), piece(own_ref, tile, h), ysend.at[0, s, h], yrecv.at[0, s, h], other(s))
+
+    def own_y_core(s, h):
+        place = piece(own_ref, came(s), h)
+        return remote(place, place, core_s.at[0, s, h], core_r.at[0, s, h], sibling)
+
+    def next_own(h):
+        return remote(source(h), piece(before_ref, tile, h), bsend.at[0, h], brecv.at[0, h], follower)
+
+    def next_y(s, h):
+        return remote(
+            piece(own_ref, came(s), h), piece(before_ref, came(s), h), bsend.at[s, h],
+            brecv.at[s, h], follower,
+        )
+
+    def before_core(s, h):
+        place = piece(before_ref, came(s) if s else tile, h)
+        return remote(place, place, core_s.at[1, s, h], core_r.at[1, s, h], sibling)
+
+    def before_y(s, h):
+        place = piece(before_ref, tile, h)
+        return remote(place, place, ysend.at[1, s, h], yrecv.at[1, s, h], other(s))
+
+    has_next = blk + 1 < blks
+    has_before = blk > 0
+    by_y = range(0, halves // 2)
+    by_x = range(halves // 2, halves)
+
+    @pl.when(blk == 0)
+    def _():
+        before_ref[...] = jnp.zeros(before_ref.shape, jnp.bfloat16)
+
+    mine = pltpu.make_async_copy(
+        hidden_ref, own_ref.at[pl.ds(pl.multiple_of(tile * tokens, tokens), tokens)], local
+    )
+    mine.start()
+    for h in range(halves):
+        for s in range(1, ways):
+            own_y(s, h).start()
+    for h in range(halves):
+
+        @pl.when(has_next)
+        def _():
+            next_own(h).start()
+
+    for h in range(halves):
+        own_core(h).start()
+
+    for h in range(halves):
+        for s in range(1, ways):
+            own_y(s, h).wait_recv()
+            own_y_core(s, h).start()
+            if h in by_x:
+
+                @pl.when(has_next)
+                def _():
+                    next_y(s, h).start()
+
+        @pl.when(has_before)
+        def _():
+            next_own(h).wait_recv()
+            before_core(0, h).start()
+            if h in by_y:
+                for s in range(1, ways):
+                    before_y(s, h).start()
+
+    @pl.when(has_before)
+    def _():
+        for s in range(1, ways):
+            for h in by_y:
+                before_y(s, h).wait_recv()
+                before_core(s, h).start()
+            for h in by_x:
+                next_y(s, h).wait_recv()
+                before_core(s, h).start()
+
+    mine.wait()
+    for h in range(halves):
+        own_core(h).wait()
+        for s in range(1, ways):
+            own_y(s, h).wait_send()
+            own_y_core(s, h).wait()
+
+        @pl.when(has_next)
+        def _():
+            next_own(h).wait_send()
+            if h in by_x:
+                for s in range(1, ways):
+                    next_y(s, h).wait_send()
+
+        @pl.when(has_before)
+        def _():
+            for s in range(ways):
+                before_core(s, h).wait()
+            if h in by_y:
+                for s in range(1, ways):
+                    before_y(s, h).wait_send()
+
+
+def spread(hidden, tiles, blks):
+    ways, halves = tiles // 2, 2
+    tokens, width = hidden.shape
+    whole = jax.ShapeDtypeStruct((tokens * tiles, width), jnp.bfloat16)
     dma = pltpu.SemaphoreType.DMA
     return pl.pallas_call(
-        functools.partial(exchange_kernel, blocks, pair, tiles),
-        out_shape=jax.ShapeDtypeStruct(kv.shape, jnp.bfloat16),
+        functools.partial(spread_kernel, (ways, halves, blks)),
+        out_shape=[whole, whole],
         in_specs=vmem_specs(1),
-        out_specs=vmem_specs(1)[0],
-        scratch_shapes=[
-            pltpu.VMEM((group,) + piece, jnp.bfloat16),
-            pltpu.VMEM((blocks,) + piece, jnp.bfloat16),
-            pltpu.VMEM(piece, jnp.float32),
-            pltpu.VMEM(piece, jnp.bfloat16),
-            pltpu.VMEM(piece, jnp.bfloat16),
-            pltpu.VMEM((group,) + piece, jnp.bfloat16),
-            dma((group,)),
-            dma((group,)),
-            dma((blocks,)),
-            dma((blocks,)),
-            dma((group,)),
-            dma((group,)),
-        ],
-        compiler_params=pltpu.CompilerParams(collective_id=0, has_side_effects=True),
-    )(kv)
-
-
-def attention_kernel(query_ref, state_ref, out_ref):
-    for head in range(HEADS):
-        queries = jnp.maximum(query_ref[:, head_columns(head)], 0)
-        both = jnp.dot(queries, state_ref[head], preferred_element_type=jnp.float32)
-        ratio = both[:, :HEAD_DIM] / (both[:, HEAD_DIM : HEAD_DIM + 1] + EPS)
-        out_ref[:, head_columns(head)] = ratio.astype(jnp.bfloat16)
+        out_specs=vmem_specs(2),
+        scratch_shapes=[dma(())]
+        + [dma((2, ways, halves))] * 4
+        + [dma((ways, halves))] * 2,
+        compiler_params=pltpu.CompilerParams(
+            collective_id=2, has_side_effects=True, vmem_limit_bytes=32 * 2**20
+        ),
+    )(hidden)
 
 
 def column_masks(stride, cols, width):
@@ -312,7 +660,9 @@
 
 
 def project_kernel(x_ref, w_ref, out_ref):
-    product = jnp.dot(x_ref[...], w_ref[...], preferred_element_type=jnp.float32)
+    product = lax.dot_general(
+        x_ref[...], w_ref[...], (((1,), (1,)), ((), ())), preferred_element_type=jnp.float32
+    )
     out_ref[...] = product.astype(jnp.bfloat16)
 
 
@@ -324,38 +674,18 @@
     tiles = lax.axis_size("tile")
     pair = BLOCK_F // frames
     blocks = lax.axis_size("blk") // pair
-    group = pair * tiles
-    per_rank = -(-HEADS // group)
     bf16 = jnp.bfloat16
 
-    w_full = lax.all_gather(w_output, "tile", axis=0, tiled=True)
-
-    kv = pl.pallas_call(
-        local_state_kernel,
-        out_shape=jax.ShapeDtypeStruct((group * per_rank, HEAD_DIM, LANES), bf16),
-        in_specs=vmem_specs(2),
-        out_specs=vmem_specs(1)[0],
-    )(key_rows.reshape(tokens, width), value_rows.reshape(tokens, width))
-    state = exchange_states(
-        kv.reshape(group, per_rank, HEAD_DIM, LANES), blocks, pair, tiles
-    ).reshape(group * per_rank, HEAD_DIM, LANES)
-    attended = pl.pallas_call(
-        attention_kernel,
-        out_shape=jax.ShapeDtypeStruct((tokens, width), bf16),
-        in_specs=vmem_specs(2),
-        out_specs=vmem_specs(1)[0],
-    )(queries.reshape(tokens, width), state)
-
-    attn_out = jnp.dot(attended, w_full, preferred_element_type=jnp.float32)
-    hidden = (stream_in.reshape(tokens, width).astype(jnp.float32) + attn_out).astype(bf16)
+    flatten = lambda x: x.reshape(tokens, width)
+    hidden, w_flat = front(
+        flatten(queries), flatten(key_rows), flatten(value_rows), flatten(stream_in), w_output,
+        w_inner, blocks, pair, tiles,
+    )
 
     chan = w_inner.shape[2]
-    w_flat = w_inner.reshape(width, 2 * chan)
     space = spatial_taps.reshape(9, 2 * chan)
     time = temporal_taps.reshape(TAPS, 2 * chan)
-    before = shifted(hidden, "blk", 1)
-    own_all = lax.all_gather(hidden, "tile", axis=0, tiled=True)
-    before_all = lax.all_gather(before, "tile", axis=0, tiled=True)
+    own_all, before_all = spread(hidden, tiles, blocks * pair)
 
     whole = tokens * tiles
     stride = frames * col_count
@@ -400,11 +730,11 @@
         out_shape=jax.ShapeDtypeStruct((whole, width), bf16),
         in_specs=[
             pl.BlockSpec((chunk, chan), lambda j: (j, 0)),
-            pl.BlockSpec((chan, width), lambda j: (0, 0)),
+            pl.BlockSpec((width, chan), lambda j: (0, 0)),
         ],
         out_specs=pl.BlockSpec((chunk, width), lambda j: (j, 0)),
         compiler_params=pltpu.CompilerParams(vmem_limit_bytes=32 * 2**20),
-    )(gated_out, w_down)
+    )(gated_out, w_down.T)
     layer_out = scatter_sum(product, hidden, tiles)
     return layer_out.reshape(queries.shape)
 

time: 245 us -> 205 us (0.84)
  Pallas kernels: 128 us -> 197 us
  waiting for transfers between devices: 63.7 us -> 0 us
  local copies, waits for them, and re-layouts: 26.8 us -> 6.6 us
  between operations: 13.2 us -> 0.15 us
  matrix products: 8.23 us -> 0 us
  starting transfers between devices: 3.36 us -> 0 us
    pallas_call x3 -> x2, Pallas kernels: 46.4 us -> 115 us  [the longest x1 70.6 us: front(): pl.pallas_call(functools.partial(front_kernel, (blocks, pair, ways, subs)...]
    all_gather x3 -> x0, waiting for transfers between devices: 36.9 us -> none  [the longest x1 36.5 us: on_device(): w_full = lax.all_gather(w_output, 'tile', axis=0, tiled=True)]
    ppermute x1 -> x0, waiting for transfers between devices: 26.1 us -> none  [shifted(): return lax.ppermute(x, axis, pairs)]
    unnamed x20, local copies, waits for them, and re-layouts: 23.6 us -> 6.6 us
    dot_general x1 -> x0, matrix products: 8.23 us -> none  [on_device(): attn_out = jnp.dot(attended, w_full, preferred_element_type=jnp.float32)]
    ppermute x1 -> x0, starting transfers between devices: 3.27 us -> none  [shifted(): return lax.ppermute(x, axis, pairs)]
  transfers between devices with their start and end apart: 4 -> 0, of which waited for: 3 -> 0; matrix products, arithmetic and copies ran while one was open for 9% -> 0% of each run, Pallas kernels for 28% -> 0%
where the time goes in v1:
time: 205 us; the launch traced here: 204 us
  Pallas kernels  197 us (96%)
  local copies, waits for them, and re-layouts  6.6 us (3%)
    pallas_call x1, Pallas kernels, front(): pl.pallas_call(functools.partial(front_kernel, (blocks, pair, ways, subs)...  70.6 us
    pallas_call x1, Pallas kernels, spread(): pl.pallas_call(functools.partial(spread_kernel, (ways, halves, blks)), ou...  44.8 us
    pallas_call x1, Pallas kernels, scatter_sum(): pl.pallas_call(functools.partial(scatter_sum_kernel, rows, chunks), out_s...  30.2 us
    pallas_call x1, Pallas kernels, on_device(): pl.pallas_call(functools.partial(gated_kernel, stride, col_count, chunk),...  24.8 us
    pallas_call x1, Pallas kernels, on_device(): pl.pallas_call(functools.partial(spatial_kernel, stride, col_count, chunk...  21.4 us
    unnamed x20, local copies, waits for them, and re-layouts  6.6 us
    pallas_call x1, Pallas kernels, on_device(): pl.pallas_call(project_kernel, grid=(whole // chunk,), out_shape=jax.Shap...  5.72 us

profile of v1, /device:TPU:9, one launch (start us, length us, event | category | flops | bytes accessed | tf_op | source)
XLA Modules:
  0.0 204.2 jit_solution(8145232730718988490)
XLA Ops:
  0.0 0.0 copy-start.4
  0.0 70.6 %shard_map.91 = (bf16[256,2240]{1,0:T(8,128)(2,1)}, bf16[2240,2048]{1,0:T(8,128)(2,1)}) custom-call(bf16[256,2240]{1,0:T(8,128)(2,1)} %bitcast.25, bf16[256,2240]{1,0:T(8,128)(2,1)} %bitcast.26, bf16[256,2240]{1,0:T(8,128)(2,1)} %bitcast.27, bf16[256,2240]{1,0:T(8,128)(2,1)} %bitcast.28, bf16[560,2240]{1,0:T(8,128)(2,1)} %w_ref.1, ...), custom_call_target="tpu_custom_call" | custom-call | tf_op jit(solution)/shard_map/pallas_call | solution.py:307
  70.6 0.0 copy-start
  70.6 1.3 copy-done
  71.8 44.8 %shard_map.92 = (bf16[1024,2240]{1,0:T(8,128)(2,1)S(1)}, bf16[1024,2240]{1,0:T(8,128)(2,1)S(1)}) custom-call(bf16[256,2240]{1,0:T(8,128)(2,1)S(1)} %copy-done), custom_call_target="tpu_custom_call" | custom-call | tf_op jit(solution)/shard_map/pallas_call | solution.py:502
  116.7 0.0 copy-start.2
  116.7 2.2 %copy-done.2 = bf16[1024,2240]{1,0:T(8,128)(2,1)} copy-done((bf16[1024,2240]{1,0:T(8,128)(2,1)}, bf16[1024,2240]{1,0:T(8,128)(2,1)S(1)}, u32[]{:S(2)}) %copy-start.2) | copy-done | bytes 4587544
  118.9 0.0 copy-done.4
  119.0 0.0 copy-start.5
  119.0 0.0 slice-start
  119.1 21.4 %shard_map.93.ov_ref.og_ref = bf16[1024,2048]{1,0:T(8,128)(2,1)S(1)} custom-call(bf16[1024,2240]{1,0:T(8,128)(2,1)S(1)} %get-tuple-element.12.hidden_ref, bf16[2240,2048]{1,0:T(8,128)(2,1)} %get-tuple-element.11.w_ref.wv_ref.wg_ref, f32[9,2048]{1,0:T(8,128)S(1)} %bitcast.20), custom_call_target="tpu_custom_call" | custom-call | flops 9395240960 | bytes 13762560 | tf_op jit(solution)/shard_map/pallas_call | solution.py:703
  140.4 0.0 copy-start.3
  140.4 2.0 copy-done.3
  142.4 0.0 copy-done.5
  142.4 0.0 slice-start.1
  142.4 24.8 %shard_map.94.x_ref = bf16[1024,1024]{1,0:T(8,128)(2,1)S(1)} custom-call(bf16[1024,2240]{1,0:T(8,128)(2,1)} %copy-done.2, bf16[2240,2048]{1,0:T(8,128)(2,1)} %get-tuple-element.11.w_ref.wv_ref.wg_ref, bf16[2240,2048]{1,0:T(8,128)(2,1)} %get-tuple-element.11.w_ref.wv_ref.wg_ref, f32[9,2048]{1,0:T(8,128)S(1)} %bitcast.21, f32[9,2048]{1,0:T(8,128)S(1)} %bitcast.22, ...), custom_call_target="tpu_custom_call" | custom-call | flops 9395240960 | bytes 13762560 | tf_op jit(solution)/shard_map/pallas_call | solution.py:713
  167.3 0.0 slice-done
  167.3 0.0 slice-done.1
  167.3 0.0 copy-start.1
  167.3 5.7 %shard_map.95 = bf16[1024,2240]{1,0:T(8,128)(2,1)S(1)} custom-call(bf16[1024,1024]{1,0:T(8,128)(2,1)S(1)} %shard_map.94.x_ref, bf16[2240,1024]{1,0:T(8,128)(2,1)S(1)} %bitcast.19), custom_call_target="tpu_custom_call" | custom-call | tf_op jit(solution)/shard_map/pallas_call | solution.py:727
  173.0 0.0 copy-done.1
  173.0 30.2 %shard_map.96 = bf16[4,64,2240]{2,1,0:T(8,128)(2,1)S(1)} custom-call(bf16[4,4,64,2240]{3,2,1,0:T(8,128)(2,1)S(1)} %bitcast.14, bf16[4,64,2240]{2,1,0:T(8,128)(2,1)S(1)} %bitcast.15), custom_call_target="tpu_custom_call" | custom-call | tf_op jit(solution)/shard_map/pallas_call | solution.py:650
  203.2 1.0 copy.13
  (4 shorter events, 0.1 us)
Async XLA Ops:
  0.0 118.9 %copy-start.4 = (f32[3,3,2,1024]{3,2,1,0:T(2,128)S(1)}, f32[3,3,2,1024]{3,2,1,0:T(2,128)}, u32[]{:S(2)}) copy-start(f32[3,3,2,1024]{3,2,1,0:T(2,128)} %param.16) | copy-start | bytes 221188
  70.6 1.3 copy-start
  116.7 2.3 %copy-start.2 = (bf16[1024,2240]{1,0:T(8,128)(2,1)}, bf16[1024,2240]{1,0:T(8,128)(2,1)S(1)}, u32[]{:S(2)}) copy-start(bf16[1024,2240]{1,0:T(8,128)(2,1)S(1)} %get-tuple-element.10.hidden_ref) | copy-start | bytes 13762564
  119.0 23.4 %copy-start.5 = (f32[3,2,1024]{2,1,0:T(2,128)S(1)}, f32[3,2,1024]{2,1,0:T(2,128)}, u32[]{:S(2)}) copy-start(f32[3,2,1024]{2,1,0:T(2,128)} %param.17) | copy-start | bytes 73732
  119.0 48.2 %slice-start = ((s8[4587520]{0:T(1024)(128)(4,1)}), s8[4194304]{0:T(1024)(128)(4,1)S(1)}, s32[]{:S(2)}) async-start(s8[4587520]{0:T(1024)(128)(4,1)} %bitcast.17), calls=%async_computation | async-start | bytes 8388608
  140.4 2.0 copy-start.3
  142.4 24.9 %slice-start.1 = ((s8[4587520]{0:T(1024)(128)(4,1)}), s8[393216]{0:T(1024)(128)(4,1)S(1)}, s32[]{:S(2)}) async-start(s8[4587520]{0:T(1024)(128)(4,1)} %bitcast.17), calls=%async_computation.1 | async-start | bytes 786432
  167.3 5.7 %copy-start.1 = (bf16[256,2240]{1,0:T(8,128)(2,1)S(1)}, bf16[256,2240]{1,0:T(8,128)(2,1)}, u32[]{:S(2)}) copy-start(bf16[256,2240]{1,0:T(8,128)(2,1)} %get-tuple-element.9.hidden_ref) | copy-start | bytes 3440644

commit v2 on v1

--- a/solution.py
+++ b/solution.py
@@ -12,6 +12,7 @@
 TAPS = 3
 BLOCK_F = 4
 LANES = 128
+FILL = 256
 EPS = 1e-06
 
 MESH = pl.DeviceIdType.MESH
@@ -347,12 +348,18 @@
     )(query, key, value, stream, w_output, w_inner)
 
 
-def spread_kernel(
-    dims, hidden_ref, own_ref, before_ref, local, core_s, core_r, ysend, yrecv, bsend, brecv,
+def layer_kernel(
+    dims, hidden_ref, flat_ref, down_ref, space_ref, time_ref, out_ref, hid, flat, down, inner,
+    gated, product, got, sums, landed, local, core_s, core_r, ysend, yrecv, bsend, brecv, psend,
+    precv, rsend, rrecv,
 ):
-    ways, halves, blks = dims
-    tokens = hidden_ref.shape[0]
+    ways, halves, blks, stride, cols = dims
+    tokens, width = hidden_ref.shape
+    tiles = 2 * ways
+    count = tokens // stride
+    chan = gated.shape[1]
     part = tokens // halves
+    bf16, f32 = jnp.bfloat16, jnp.float32
     blk = lax.axis_index("blk")
     tile = lax.axis_index("tile")
     core = tile % 2
@@ -366,8 +373,22 @@
             device_id_type=MESH,
         )
 
-    def other(s):
-        return (blk, ((y + s) % ways) * 2 + core)
+    def lanes_at(c):
+        return pl.ds(pl.multiple_of(c * FILL, FILL), FILL)
+
+    def flat_copy(c):
+        return pltpu.make_async_copy(
+            flat_ref.at[:, lanes_at(c)], flat.at[:, lanes_at(c)], local.at[c + 1]
+        )
+
+    fills = 2 * chan // FILL
+    for c in range(fills):
+        flat_copy(c).start()
+    down_copy = pltpu.make_async_copy(down_ref, down, local.at[0])
+    down_copy.start()
+
+    def there(s):
+        return (y + s) % ways
 
     def came(s):
         return ((y + ways - s) % ways) * 2 + core
@@ -375,295 +396,344 @@
     barrier = pltpu.get_barrier_semaphore()
     pl.semaphore_signal(barrier, inc=1, device_id=sibling, device_id_type=MESH)
     for s in range(1, ways):
-        pl.semaphore_signal(barrier, inc=1, device_id=other(s), device_id_type=MESH)
+        pl.semaphore_signal(
+            barrier, inc=1, device_id=(blk, there(s) * 2 + core), device_id_type=MESH
+        )
     pl.semaphore_signal(barrier, inc=1, device_id=follower, device_id_type=MESH)
     pl.semaphore_signal(
         barrier, inc=1, device_id=((blk + blks - 1) % blks, tile), device_id_type=MESH
     )
     pl.semaphore_wait(barrier, ways + 2)
 
-    def rows_at(t, h):
-        return pl.ds(pl.multiple_of(t * tokens + h * part, part), part)
-
-    def piece(ref, t, h):
-        return ref.at[rows_at(t, h)]
+    def piece(which, t, h):
+        return hid.at[which, t, pl.ds(h * part, part)]
 
     def source(h):
         return hidden_ref.at[pl.ds(h * part, part)]
 
     def own_core(h):
-        return remote(source(h), piece(own_ref, tile, h), core_s.at[0, 0, h], core_r.at[0, 0, h], sibling)
+        return remote(
+            source(h), piece(0, tile, h), core_s.at[0, 0, h], core_r.at[0, 0, h], sibling
+        )
 
     def own_y(s, h):
-        return remote(source(h), piece(own_ref, tile, h), ysend.at[0, s, h], yrecv.at[0, s, h], other(s))
+        return remote(
+            source(h), piece(0, tile, h), ysend.at[0, s, h], yrecv.at[0, s, h],
+            (blk, there(s) * 2 + core),
+        )
 
     def own_y_core(s, h):
-        place = piece(own_ref, came(s), h)
+        place = piece(0, came(s), h)
         return remote(place, place, core_s.at[0, s, h], core_r.at[0, s, h], sibling)
 
     def next_own(h):
-        return remote(source(h), piece(before_ref, tile, h), bsend.at[0, h], brecv.at[0, h], follower)
+        return remote(source(h), piece(1, tile, h), bsend.at[0, h], brecv.at[0, h], follower)
 
     def next_y(s, h):
         return remote(
-            piece(own_ref, came(s), h), piece(before_ref, came(s), h), bsend.at[s, h],
-            brecv.at[s, h], follower,
+            piece(0, came(s), h), piece(1, came(s), h), bsend.at[s, h], brecv.at[s, h], follower
         )
 
     def before_core(s, h):
-        place = piece(before_ref, came(s) if s else tile, h)
+        place = piece(1, came(s), h)
         return remote(place, place, core_s.at[1, s, h], core_r.at[1, s, h], sibling)
 
     def before_y(s, h):
-        place = piece(before_ref, tile, h)
-        return remote(place, place, ysend.at[1, s, h], yrecv.at[1, s, h], other(s))
+        place = piece(1, tile, h)
+        return remote(
+            place, place, ysend.at[1, s, h], yrecv.at[1, s, h], (blk, there(s) * 2 + core)
+        )
+
+    def to_core(s, t):
+        return remote(product.at[t], got.at[s], psend.at[s], precv.at[s], sibling)
+
+    def to_y(s):
+        return remote(
+            sums.at[s], landed.at[s], rsend.at[s], rrecv.at[s], (blk, there(s) * 2 + core)
+        )
 
     has_next = blk + 1 < blks
     has_before = blk > 0
     by_y = range(0, halves // 2)
-    by_x = range(halves // 2, halves)
+    others = range(1, ways)
+    every = range(halves)
+
+    @pl.when(core == 0)
+    def _():
+        for h in every:
+            for s in others:
+                own_y(s, h).start()
+
+    @pl.when(jnp.logical_and(core == 1, has_next))
+    def _():
+        for h in every:
+            next_own(h).start()
+
+    for h in every:
+        own_core(h).start()
+
+    edge = jnp.zeros((stride, 2 * chan), bf16)
+    for which in range(2):
+        inner[which, 0:stride] = edge
+        inner[which, stride + tiles * tokens : 2 * stride + tiles * tokens] = edge
 
     @pl.when(blk == 0)
     def _():
-        before_ref[...] = jnp.zeros(before_ref.shape, jnp.bfloat16)
-
-    mine = pltpu.make_async_copy(
-        hidden_ref, own_ref.at[pl.ds(pl.multiple_of(tile * tokens, tokens), tokens)], local
-    )
-    mine.start()
-    for h in range(halves):
-        for s in range(1, ways):
-            own_y(s, h).start()
-    for h in range(halves):
-
+        for t in range(tiles):
+            hid[1, t] = jnp.zeros((tokens, width), bf16)
+
+    def fill(load, which, t, first=False):
+        start = pl.multiple_of((t * count + 1) * stride, stride)
+
+        def body(c, carry):
+            if first:
+                flat_copy(c).wait()
+            result = jnp.dot(load(), flat[:, lanes_at(c)], preferred_element_type=f32)
+            inner[which, pl.ds(start, tokens), lanes_at(c)] = jax.nn.silu(result).astype(bf16)
+            return carry
+
+        lax.fori_loop(0, fills, body, 0)
+
+    def fill_from(which, t):
+        fill(lambda: hid[which, t], which, t)
+
+    fill(lambda: hidden_ref[...], 0, tile, True)
+    for h in every:
+        own_core(h).wait_recv()
+    fill_from(0, y * 2 + 1 - core)
+
+    def take_own():
+        for h in every:
+            for s in others:
+                own_y(s, h).wait_recv()
+                own_y_core(s, h).start()
+                if h not in by_y:
+                    pl.when(has_next)(next_y(s, h).start)
+
+    def take_before():
+        @pl.when(has_before)
+        def _():
+            for h in every:
+                next_own(h).wait_recv()
+                before_core(0, h).start()
+                if h in by_y:
+                    for s in others:
+                        before_y(s, h).start()
+
+    def forwarded_own():
+        for h in every:
+            for s in others:
+                own_y_core(s, h).wait_recv()
+
+    def forwarded_before():
+        @pl.when(has_before)
+        def _():
+            for h in every:
+                before_core(0, h).wait_recv()
+
+    @pl.when(core == 0)
+    def _():
         @pl.when(has_next)
         def _():
-            next_own(h).start()
-
-    for h in range(halves):
-        own_core(h).start()
-
-    for h in range(halves):
-        for s in range(1, ways):
-            own_y(s, h).wait_recv()
-            own_y_core(s, h).start()
-            if h in by_x:
-
-                @pl.when(has_next)
-                def _():
-                    next_y(s, h).start()
-
-        @pl.when(has_before)
-        def _():
-            next_own(h).wait_recv()
-            before_core(0, h).start()
-            if h in by_y:
-                for s in range(1, ways):
-                    before_y(s, h).start()
+            for h in every:
+                next_own(h).start()
+
+        take_own()
+
+    @pl.when(core == 1)
+    def _():
+        for h in every:
+            for s in others:
+                own_y(s, h).start()
+        take_before()
+
+    pl.when(core == 0)(forwarded_before)
+    pl.when(core == 1)(forwarded_own)
+    for s in others:
+        fill_from(0, there(s) * 2)
+    fill_from(1, y * 2 + 1)
+
+    @pl.when(core == 0)
+    def _():
+        take_before()
+        forwarded_own()
+
+    @pl.when(core == 1)
+    def _():
+        take_own()
+        forwarded_before()
+
+    fill_from(1, y * 2)
+    for s in others:
+        fill_from(0, there(s) * 2 + 1)
+
+    col = lax.broadcasted_iota(jnp.int32, (stride, LANES), 0) % cols
+    masks = (col > 0, col < cols - 1)
+
+    def mix(t):
+        base = t * count
+
+        def body(c, carry):
+            def mixed(lanes):
+                taps = [space_ref[k : k + 1, lanes] for k in range(9)]
+                times = [time_ref[k : k + 1, lanes] for k in range(TAPS)]
+
+                def spatial(which, row):
+                    loads = [
+                        inner[
+                            which, pl.ds(pl.multiple_of((base + row + a) * stride, stride), stride),
+                            lanes,
+                        ].astype(f32)
+                        for a in range(3)
+                    ]
+                    parts = [
+                        sum(loads[a] * taps[3 * a + b] for a in range(3)) for b in range(3)
+                    ]
+                    left = jnp.where(masks[0], pltpu.roll(parts[0], 1, 0), 0.0)
+                    right = jnp.where(masks[1], pltpu.roll(parts[2], stride - 1, 0), 0.0)
+                    return (parts[1] + left + right).astype(bf16).astype(f32)
+
+                def over_time(row):
+                    long = jnp.concatenate([spatial(1, row), spatial(0, row)], axis=0)
+                    mixed_row = long[stride:] * times[0]
+                    for lag in range(1, TAPS):
+                        start = stride - lag * cols
+                        mixed_row = mixed_row + long[start : start + stride] * times[lag]
+                    return mixed_row
+
+                return over_time
+
+            value = mixed(pl.ds(pl.multiple_of(c * LANES, LANES), LANES))
+            gate = mixed(pl.ds(pl.multiple_of(chan + c * LANES, LANES), LANES))
+            for row in range(count):
+                gated[row * stride : (row + 1) * stride, pl.ds(pl.multiple_of(c * LANES, LANES), LANES)] = (
+                    value(row) * jax.nn.silu(gate(row))
+                ).astype(bf16)
+            return carry
+
+        lax.fori_loop(0, chan // LANES, body, 0)
+        result = lax.dot_general(
+            gated[...], down[...], (((1,), (1,)), ((), ())), preferred_element_type=f32
+        )
+        product[t] = result.astype(bf16)
+
+    def own_rows(t):
+        mix(t)
+        pl.when(core != t % 2)(to_core(0, t).start)
+
+    down_copy.wait()
+    early = [y * (tiles - 1)] if ways == 2 else []
+    late = [1 + y] if ways == 2 else [y * 2, y * 2 + 1]
+    for t in early:
+        own_rows(t)
 
     @pl.when(has_before)
     def _():
-        for s in range(1, ways):
-            for h in by_y:
-                before_y(s, h).wait_recv()
+        for s in others:
+            for h in every:
+                if h in by_y:
+                    before_y(s, h).wait_recv()
+                else:
+                    next_y(s, h).wait_recv()
                 before_core(s, h).start()
-            for h in by_x:
-                next_y(s, h).wait_recv()
-                before_core(s, h).start()
-
-    mine.wait()
-    for h in range(halves):
-        own_core(h).wait()
-        for s in range(1, ways):
+
+    for s in others:
+        fill_from(1, there(s) * 2 + core)
+
+    @pl.when(has_before)
+    def _():
+        for s in others:
+            for h in every:
+                before_core(s, h).wait_recv()
+
+    for s in others:
+        fill_from(1, there(s) * 2 + 1 - core)
+
+    for s in others:
+        for c in range(2):
+            t = there(s) * 2 + c
+            mix(t)
+            pl.when(core != c)(to_core(s, t).start)
+
+            @pl.when(core == c)
+            def _():
+                to_core(s, t).wait_recv()
+                sums[s] = (product[t].astype(f32) + got[s].astype(f32)).astype(bf16)
+                to_y(s).start()
+
+    for t in late:
+        own_rows(t)
+    to_core(0, tile).wait_recv()
+    for s in others:
+        to_y(s).wait_recv()
+    for start in range(0, tokens, stride):
+        where = slice(start, start + stride)
+        total = product[tile, where].astype(f32) + got[0, where].astype(f32)
+        for s in others:
+            total = total + landed[s, where].astype(f32)
+        out_ref[where] = (hidden_ref[where].astype(f32) + total).astype(bf16)
+
+    for h in every:
+        own_core(h).wait_send()
+        for s in others:
             own_y(s, h).wait_send()
-            own_y_core(s, h).wait()
+            own_y_core(s, h).wait_send()
 
         @pl.when(has_next)
         def _():
             next_own(h).wait_send()
-            if h in by_x:
-                for s in range(1, ways):
+            if h not in by_y:
+                for s in others:
                     next_y(s, h).wait_send()
 
         @pl.when(has_before)
         def _():
             for s in range(ways):
-                before_core(s, h).wait()
+                before_core(s, h).wait_send()
             if h in by_y:
-                for s in range(1, ways):
+                for s in others:
                     before_y(s, h).wait_send()
 
-
-def spread(hidden, tiles, blks):
+    for s in range(ways):
+        to_core(s, tile).wait_send()
+    for s in others:
+        to_y(s).wait_send()
+
+
+def finish(hidden, flat, down, space, time, tiles, blks, stride, cols):
     ways, halves = tiles // 2, 2
     tokens, width = hidden.shape
-    whole = jax.ShapeDtypeStruct((tokens * tiles, width), jnp.bfloat16)
+    chan = flat.shape[1] // 2
+    bf16 = jnp.bfloat16
     dma = pltpu.SemaphoreType.DMA
+    vmem = pltpu.VMEM
+    piece = (tokens, width)
+    inside = pl.BlockSpec(memory_space=pltpu.VMEM)
+    anywhere = pl.BlockSpec(memory_space=pl.ANY)
     return pl.pallas_call(
-        functools.partial(spread_kernel, (ways, halves, blks)),
-        out_shape=[whole, whole],
-        in_specs=vmem_specs(1),
-        out_specs=vmem_specs(2),
-        scratch_shapes=[dma(())]
+        functools.partial(layer_kernel, (ways, halves, blks, stride, cols)),
+        out_shape=jax.ShapeDtypeStruct(piece, bf16),
+        in_specs=[inside, anywhere, anywhere, inside, inside],
+        out_specs=inside,
+        scratch_shapes=[
+            vmem((2, tiles) + piece, bf16),
+            vmem(flat.shape, bf16),
+            vmem(down.shape, bf16),
+            vmem((2, tiles * tokens + 2 * stride, 2 * chan), bf16),
+            vmem((tokens, chan), bf16),
+            vmem((tiles,) + piece, bf16),
+            vmem((ways,) + piece, bf16),
+            vmem((ways,) + piece, bf16),
+            vmem((ways,) + piece, bf16),
+            dma((1 + 2 * chan // FILL,)),
+        ]
         + [dma((2, ways, halves))] * 4
-        + [dma((ways, halves))] * 2,
+        + [dma((ways, halves))] * 2
+        + [dma((ways,))] * 4,
         compiler_params=pltpu.CompilerParams(
-            collective_id=2, has_side_effects=True, vmem_limit_bytes=32 * 2**20
+            collective_id=1, has_side_effects=True, vmem_limit_bytes=61 * 2**20
         ),
-    )(hidden)
-
-
-def column_masks(stride, cols, width):
-    col = lax.broadcasted_iota(jnp.int32, (stride, width), 0) % cols
-    return col > 0, col < cols - 1
-
-
-def fill_inner(hidden_ref, w_ref, inner, stride, chunk):
-    tokens = hidden_ref.shape[0]
-    edge = jnp.zeros((stride, inner.shape[1]), jnp.bfloat16)
-    inner[:stride] = edge
-    inner[stride + tokens :] = edge
-    for start in range(0, tokens, chunk):
-        product = jnp.dot(
-            hidden_ref[start : start + chunk], w_ref[...], preferred_element_type=jnp.float32
-        )
-        inner[stride + start : stride + start + chunk] = jax.nn.silu(product).astype(jnp.bfloat16)
-
-
-def conv_row(inner, taps_ref, row, stride, masks):
-    rows = [
-        inner[pl.ds(pl.multiple_of((row + a) * stride, stride), stride)].astype(jnp.float32)
-        for a in range(3)
-    ]
-    sums = [
-        sum(rows[a] * taps_ref[3 * a + b : 3 * a + b + 1] for a in range(3)) for b in range(3)
-    ]
-    from_left = jnp.where(masks[0], pltpu.roll(sums[0], 1, 0), 0.0)
-    from_right = jnp.where(masks[1], pltpu.roll(sums[2], stride - 1, 0), 0.0)
-    return sums[1] + from_left + from_right
-
-
-def spatial_kernel(stride, cols, chunk, hidden_ref, w_ref, taps_ref, out_ref, inner):
-    fill_inner(hidden_ref, w_ref, inner, stride, chunk)
-    masks = column_masks(stride, cols, inner.shape[1])
-
-    def body(row, carry):
-        value = conv_row(inner, taps_ref, row, stride, masks)
-        out_ref[pl.ds(pl.multiple_of(row * stride, stride), stride)] = value.astype(jnp.bfloat16)
-        return carry
-
-    lax.fori_loop(0, hidden_ref.shape[0] // stride, body, 0, unroll=2)
-
-
-def gated_kernel(
-    stride, cols, chunk, hidden_ref, wv_ref, wg_ref, sv_ref, sg_ref, tv_ref, tg_ref, ov_ref, og_ref,
-    out_ref, inner_v, inner_g,
-):
-    fill_inner(hidden_ref, wv_ref, inner_v, stride, chunk)
-    fill_inner(hidden_ref, wg_ref, inner_g, stride, chunk)
-    masks = column_masks(stride, cols, inner_v.shape[1])
-
-    def mixed(inner, taps_ref, time_ref, own_ref, row, where):
-        before = conv_row(inner, taps_ref, row, stride, masks)
-        before = before.astype(jnp.bfloat16).astype(jnp.float32)
-        extended = jnp.concatenate([before, own_ref[where].astype(jnp.float32)], axis=0)
-        total = extended[stride:] * time_ref[0:1]
-        for lag in range(1, TAPS):
-            start = stride - lag * cols
-            total = total + extended[start : start + stride] * time_ref[lag : lag + 1]
-        return total
-
-    def body(row, carry):
-        where = pl.ds(pl.multiple_of(row * stride, stride), stride)
-        value = mixed(inner_v, sv_ref, tv_ref, ov_ref, row, where)
-        gate = mixed(inner_g, sg_ref, tg_ref, og_ref, row, where)
-        out_ref[where] = (value * jax.nn.silu(gate)).astype(jnp.bfloat16)
-        return carry
-
-    lax.fori_loop(0, hidden_ref.shape[0] // stride, body, 0)
-
-
-def scatter_sum_kernel(
-    rows, chunks, product_ref, hidden_ref, out_ref, got, sums, landed, send1, recv1, send2, recv2
-):
-    blk = lax.axis_index("blk")
-    tile = lax.axis_index("tile")
-    core = tile % 2
-    y = tile // 2
-    order = [step % rows for step in range(1, rows + 1)]
-
-    barrier = pltpu.get_barrier_semaphore()
-    pl.semaphore_signal(barrier, inc=1, device_id=(blk, y * 2 + 1 - core), device_id_type=MESH)
-    for step in range(1, rows):
-        pl.semaphore_signal(
-            barrier, inc=1, device_id=(blk, ((y + step) % rows) * 2 + core), device_id_type=MESH
-        )
-    pl.semaphore_wait(barrier, rows)
-
-    first = {}
-    for step in order:
-        there = (y + step) % rows
-        for k in range(chunks):
-            slot = step * chunks + k
-            copy = pltpu.make_async_remote_copy(
-                src_ref=product_ref.at[there * 2 + 1 - core, k], dst_ref=got.at[step, k],
-                send_sem=send1.at[slot], recv_sem=recv1.at[slot],
-                device_id=(blk, y * 2 + 1 - core), device_id_type=MESH,
-            )
-            copy.start()
-            first[step, k] = copy
-    second = {}
-    for k in range(chunks):
-        for step in range(1, rows):
-            there = (y + step) % rows
-            slot = step * chunks + k
-            first[step, k].wait_recv()
-            chip = product_ref[there * 2 + core, k].astype(jnp.float32) + got[step, k].astype(
-                jnp.float32
-            )
-            sums[step, k] = chip.astype(jnp.bfloat16)
-            copy = pltpu.make_async_remote_copy(
-                src_ref=sums.at[step, k], dst_ref=landed.at[step, k],
-                send_sem=send2.at[slot], recv_sem=recv2.at[slot],
-                device_id=(blk, there * 2 + core), device_id_type=MESH,
-            )
-            copy.start()
-            second[step, k] = copy
-    for k in range(chunks):
-        first[0, k].wait_recv()
-        total = product_ref[tile, k].astype(jnp.float32) + got[0, k].astype(jnp.float32)
-        for step in range(1, rows):
-            second[step, k].wait_recv()
-            total = total + landed[step, k].astype(jnp.float32)
-        out_ref[k] = (hidden_ref[k].astype(jnp.float32) + total).astype(jnp.bfloat16)
-    for copy in list(first.values()) + list(second.values()):
-        copy.wait_send()
-
-
-def scatter_sum(product, hidden, tiles):
-    rows = tiles // 2
-    chunks = 4
-    tokens, width = hidden.shape
-    piece = (chunks, tokens // chunks, width)
-    bf16 = jnp.bfloat16
-    sems = [pltpu.SemaphoreType.DMA((rows * chunks,))] * 4
-    return pl.pallas_call(
-        functools.partial(scatter_sum_kernel, rows, chunks),
-        out_shape=jax.ShapeDtypeStruct(piece, bf16),
-        in_specs=vmem_specs(2),
-        out_specs=vmem_specs(1)[0],
-        scratch_shapes=[pltpu.VMEM((rows,) + piece, bf16)] * 3 + sems,
-        compiler_params=pltpu.CompilerParams(
-            collective_id=1, has_side_effects=True, vmem_limit_bytes=40 * 2**20
-        ),
-    )(product.reshape((tiles,) + piece), hidden.reshape(piece))
-
-
-def project_kernel(x_ref, w_ref, out_ref):
-    product = lax.dot_general(
-        x_ref[...], w_ref[...], (((1,), (1,)), ((), ())), preferred_element_type=jnp.float32
-    )
-    out_ref[...] = product.astype(jnp.bfloat16)
+    )(hidden, flat, down, space, time)
 
 
 def on_device(
@@ -685,57 +755,9 @@
     chan = w_inner.shape[2]
     space = spatial_taps.reshape(9, 2 * chan)
     time = temporal_taps.reshape(TAPS, 2 * chan)
-    own_all, before_all = spread(hidden, tiles, blocks * pair)
-
-    whole = tokens * tiles
-    stride = frames * col_count
-    lane_block = 256
-    chunk = 256
-    value_blocks = chan // lane_block
-    full = lambda rows: pl.BlockSpec((rows, width), lambda j: (0, 0))
-    block = lambda rows: pl.BlockSpec((rows, lane_block), lambda j: (0, j))
-    gate = lambda rows: pl.BlockSpec((rows, lane_block), lambda j: (0, j + value_blocks))
-    inner_scratch = pltpu.VMEM((whole + 2 * stride, lane_block), bf16)
-    flops = 2 * whole * width * 2 * chan
-    cost = pl.CostEstimate(
-        flops=flops, bytes_accessed=2 * (whole * width + 2 * width * chan), transcendentals=0
+    layer_out = finish(
+        hidden, w_flat, w_down.T, space, time, tiles, blocks * pair, frames * col_count, col_count
     )
-    spatial = pl.pallas_call(
-        functools.partial(spatial_kernel, stride, col_count, chunk),
-        grid=(2 * value_blocks,),
-        out_shape=jax.ShapeDtypeStruct((whole, 2 * chan), bf16),
-        in_specs=[full(whole), block(width), block(9)],
-        out_specs=block(whole),
-        scratch_shapes=[inner_scratch],
-        cost_estimate=cost,
-        compiler_params=pltpu.CompilerParams(vmem_limit_bytes=40 * 2**20),
-    )(own_all, w_flat, space)
-    gated_out = pl.pallas_call(
-        functools.partial(gated_kernel, stride, col_count, chunk),
-        grid=(value_blocks,),
-        out_shape=jax.ShapeDtypeStruct((whole, chan), bf16),
-        in_specs=[
-            full(whole), block(width), gate(width), block(9), gate(9), block(TAPS), gate(TAPS),
-            block(whole), gate(whole),
-        ],
-        out_specs=block(whole),
-        scratch_shapes=[inner_scratch, inner_scratch],
-        cost_estimate=cost,
-        compiler_params=pltpu.CompilerParams(vmem_limit_bytes=48 * 2**20),
-    )(before_all, w_flat, w_flat, space, space, time, time, spatial, spatial)
-
-    product = pl.pallas_call(
-        project_kernel,
-        grid=(whole // chunk,),
-        out_shape=jax.ShapeDtypeStruct((whole, width), bf16),
-        in_specs=[
-            pl.BlockSpec((chunk, chan), lambda j: (j, 0)),
-            pl.BlockSpec((width, chan), lambda j: (0, 0)),
-        ],
-        out_specs=pl.BlockSpec((chunk, width), lambda j: (j, 0)),
-        compiler_params=pltpu.CompilerParams(vmem_limit_bytes=32 * 2**20),
-    )(gated_out, w_down.T)
-    layer_out = scatter_sum(product, hidden, tiles)
     return layer_out.reshape(queries.shape)
 
 

time: 205 us -> 171 us (0.83)
  Pallas kernels: 197 us -> 166 us
    pallas_call x5 -> x1, Pallas kernels: 127 us -> 95.2 us  [finish(): pl.pallas_call(functools.partial(layer_kernel, (ways, halves, blks, strid...]
    unnamed x20 -> x4, local copies, waits for them, and re-layouts: 6.6 us -> 5.34 us
where the time goes in v2:
time: 171 us
  Pallas kernels  166 us (97%)
  local copies, waits for them, and re-layouts  5.34 us (3%)
    pallas_call x1, Pallas kernels, finish(): pl.pallas_call(functools.partial(layer_kernel, (ways, halves, blks, strid...  95.2 us
    pallas_call x1, Pallas kernels, front(): pl.pallas_call(functools.partial(front_kernel, (blocks, pair, ways, subs)...  70.5 us
    unnamed x4, local copies, waits for them, and re-layouts  5.34 us

profile of v2, /device:TPU:9, one launch (start us, length us, event | category | flops | bytes accessed | tf_op | source)
XLA Modules:
  0.0 171.1 jit_solution(7863560836566471739)
XLA Ops:
  0.0 1.4 copy.11
  1.4 0.9 pad
  2.3 0.7 copy.10
  3.0 70.5 %shard_map.91 = (bf16[256,2240]{1,0:T(8,128)(2,1)}, bf16[2240,2048]{1,0:T(8,128)(2,1)}) custom-call(bf16[256,2240]{1,0:T(8,128)(2,1)} %bitcast.14, bf16[256,2240]{1,0:T(8,128)(2,1)} %bitcast.15, bf16[256,2240]{1,0:T(8,128)(2,1)} %bitcast.16, bf16[256,2240]{1,0:T(8,128)(2,1)} %bitcast.17, bf16[560,2240]{1,0:T(8,128)(2,1)} %w_ref.1, ...), custom_call_target="tpu_custom_call" | custom-call | tf_op jit(solution)/shard_map/pallas_call | solution.py:308
  73.5 95.2 %shard_map.92 = bf16[256,2240]{1,0:T(8,128)(2,1)} custom-call(bf16[256,2240]{1,0:T(8,128)(2,1)} %get-tuple-element.7.hidden_ref, bf16[2240,2048]{1,0:T(8,128)(2,1)} %get-tuple-element.8.flat_ref, bf16[2240,1024]{1,0:T(8,128)(2,1)} %bitcast.13, f32[9,2048]{1,0:T(8,128)} %bitcast.18, f32[3,2048]{1,0:T(4,128)} %bitcast.20), custom_call_target="tpu_custom_call" | custom-call | tf_op jit(solution)/shard_map/pallas_call | solution.py:713
  168.8 2.4 %copy.13 = bf16[8,2,16,2240]{3,2,1,0:T(8,128)(2,1)} copy(bf16[8,2,16,2240]{3,2,1,0:T(8,128)(2,1)} %bitcast.12) | data formatting | bytes 2293760

commit v3 on v2

--- a/solution.py
+++ b/solution.py
@@ -53,7 +53,11 @@
     member = blk % pair
     rank = member * ways + y
     sibling = (blk, y * 2 + 1 - core)
-    ids = pair * subs
+    assert pair == 2 and blocks % 2 == 0
+    ids = 4 * subs
+    quarter = member * 2 + block % 2
+    beside = (block * pair + 1 - member, tile)
+    across = ((block + 1 - 2 * (block % 2)) * pair + member, tile)
 
     def remote(src, dst, send, recv, device):
         return pltpu.make_async_remote_copy(
@@ -94,12 +98,11 @@
     def came(s):
         return ((y + ways - s) % ways) * 2 + core
 
-    def x_send(s, j, st, i):
-        part = rows_of(i * subs + j, ids, rows)
+    def side_send(way, s, j, i):
+        part = rows_of(i * subs + j % subs, ids, rows)
         place = wbuf.at[came(s), part]
         return remote(
-            place, place, xsend.at[st, s, j], xrecv.at[st, s, j],
-            (block * pair + (member + st) % pair, tile),
+            place, place, xsend.at[way, s, j], xrecv.at[way, s, j], across if way else beside
         )
 
     def core_send(s, number):
@@ -107,38 +110,65 @@
         place = wbuf.at[came(s), part]
         return remote(place, place, csend.at[s, number], crecv.at[s, number], sibling)
 
-    def each_member(body):
-        for i in range(pair):
-            pl.when(member == i)(functools.partial(body, i))
+    def each_quarter(body):
+        for i in range(4):
+            pl.when(quarter == i)(functools.partial(body, i))
 
     def start_y(j):
         def body(i):
             for s in range(1, ways):
                 y_send(s, j, i).start()
 
-        each_member(body)
+        each_quarter(body)
 
     def relay_y(j):
         def body(i):
             for s in range(1, ways):
                 y_send(s, j, i).wait_recv()
-                for st in range(1, pair):
-                    x_send(s, j, st, i).start()
+                for way in range(2):
+                    side_send(way, s, j, i).start()
                 core_send(s, i * subs + j).start()
 
-        each_member(body)
-
-    def relay_x(j):
+        each_quarter(body)
+
+    def relay_side(j):
+        def body(i):
+            sources = (i ^ 2, i ^ 1)
+            for s in range(1, ways):
+                for way in range(2):
+                    source = sources[way]
+                    side_send(way, s, j, source).wait_recv()
+                    if way != j % 2:
+                        side_send(1 - way, s, subs + j, source).start()
+                    core_send(s, source * subs + j).start()
+
+        each_quarter(body)
+
+    def relay_last(j):
         def body(i):
             for s in range(1, ways):
-                for st in range(1, pair):
-                    source = (i + pair - st) % pair
-                    x_send(s, j, st, source).wait_recv()
-                    core_send(s, source * subs + j).start()
-
-        each_member(body)
+                side_send(j % 2, s, subs + j, i ^ 3).wait_recv()
+                core_send(s, (i ^ 3) * subs + j).start()
+
+        each_quarter(body)
 
     start_y(0)
+
+    rows_in, steps = 64, width // 64
+    place_of = lax.broadcasted_iota(jnp.int32, (rows_in, 2 * rows_in), 0) * 2
+    here = lax.broadcasted_iota(jnp.int32, (rows_in, 2 * rows_in), 1)
+    picks = [(here == place_of + kind).astype(jnp.bfloat16) for kind in range(2)]
+
+    def deinterleave(start, count):
+        def body(n, carry):
+            where = pl.ds(pl.multiple_of(n * rows_in, rows_in), rows_in)
+            both = raw[where].reshape(2 * rows_in, chan)
+            for kind in range(2):
+                picked = jnp.dot(picks[kind], both, preferred_element_type=jnp.float32)
+                flat[where, kind * chan : (kind + 1) * chan] = picked.astype(jnp.bfloat16)
+            return carry
+
+        lax.fori_loop(start, start + count, body, 0)
 
     ones = jnp.ones((tokens, LANES - HEAD_DIM), jnp.bfloat16)
     slots = group * per_rank
@@ -157,7 +187,8 @@
 
     kv_core = remote(kv.at[1 - core], got0, core_s.at[1], core_r.at[1], sibling)
     kv_core.start()
-    relay_y(0)
+    raw_copy.wait()
+    deinterleave(0, 4)
     kv_core.wait_recv()
     for r in range(group):
         csum[r] = (kv[core, r].astype(jnp.float32) + got0[r].astype(jnp.float32)).astype(
@@ -170,6 +201,7 @@
         copy.start()
         first.append(copy)
     start_y(1)
+    deinterleave(4, 8)
     total[...] = kv[core, rank].astype(jnp.float32) + got0[rank].astype(jnp.float32)
     for step in range(1, group):
         first[step - 1].wait_recv()
@@ -187,26 +219,11 @@
         def _():
             later(step).start()
 
-    raw_copy.wait()
-
-    def deinterleave(start, count):
-        def body(n, carry):
-            where = pl.ds(pl.multiple_of(n * 64, 64), 64)
-            both = raw[where]
-            flat[where, 0:chan] = both[:, 0, :]
-            flat[where, chan : 2 * chan] = both[:, 1, :]
-            return carry
-
-        lax.fori_loop(start, start + count, body, 0)
-
-    steps = width // 64
-    deinterleave(0, steps // 2)
+    relay_y(0)
+    deinterleave(12, 10)
     relay_y(1)
-    start_y(2)
-    relay_x(0)
-    deinterleave(steps // 2, steps - steps // 2)
-    flat_copy = pltpu.make_async_copy(flat, flat_ref, local.at[2])
-    flat_copy.start()
+    deinterleave(22, 4)
+    relay_side(0)
 
     for step in range(1, blocks):
 
@@ -226,15 +243,16 @@
     fourth = [remote(final_send, state.at[core, rank], send4.at[0], recv4.at[0], sibling)]
     fourth[0].start()
     state[core, rank] = total[...].astype(jnp.bfloat16)
-    relay_y(2)
-    start_y(3)
-    relay_x(1)
+    deinterleave(26, steps - 26)
+    flat_copy = pltpu.make_async_copy(flat, flat_ref, local.at[2])
+    flat_copy.start()
     for step in range(1, group):
         third[step - 1].wait_recv()
         place = state.at[core, (rank + group - step) % group]
         copy = remote(place, place, send4.at[step], recv4.at[step], sibling)
         copy.start()
         fourth.append(copy)
+    relay_side(1)
     for copy in fourth:
         copy.wait_recv()
 
@@ -246,8 +264,8 @@
         )
         ratio = both[:, :HEAD_DIM] / (both[:, HEAD_DIM : HEAD_DIM + 1] + EPS)
         attended[:, head_columns(head)] = ratio.astype(jnp.bfloat16)
-    relay_y(3)
-    relay_x(2)
+    relay_last(0)
+    relay_last(1)
     for t in range(2 * ways):
         pieces[t] = attended[:, t * rows : (t + 1) * rows]
 
@@ -261,7 +279,6 @@
     own_copy.wait()
     w_core.wait_recv()
     lax.fori_loop(0, 2, add_piece, 0)
-    relay_x(3)
     for s in range(1, ways):
         for number in range(ids):
             core_send(s, number).wait_recv()
@@ -280,20 +297,22 @@
             later(step).wait_send()
 
     def sent(i):
+        sources = (i ^ 2, i ^ 1)
         for s in range(1, ways):
             for j in range(subs):
                 y_send(s, j, i).wait_send()
-                for st in range(1, pair):
-                    x_send(s, j, st, i).wait_send()
-
-    each_member(sent)
+                for way in range(2):
+                    side_send(way, s, j, i).wait_send()
+                side_send(j % 2, s, subs + j, sources[1 - j % 2]).wait_send()
+
+    each_quarter(sent)
     for s in range(1, ways):
         for number in range(ids):
             core_send(s, number).wait_send()
 
 
 def front(query, key, value, stream, w_output, w_inner, blocks, pair, tiles):
-    ways, subs = tiles // 2, 4
+    ways, subs = tiles // 2, 2
     group = pair * ways
     per_rank = -(-(-(-HEADS // 2)) // group)
     tokens, width = query.shape
@@ -334,10 +353,10 @@
             dma((2,)),
             dma((ways, subs)),
             dma((ways, subs)),
-            dma((pair, ways, subs)),
-            dma((pair, ways, subs)),
-            dma((ways, pair * subs)),
-            dma((ways, pair * subs)),
+            dma((2, ways, 2 * subs)),
+            dma((2, ways, 2 * subs)),
+            dma((ways, 4 * subs)),
+            dma((ways, 4 * subs)),
         ]
         + [dma((group,))] * 2
         + [dma((blocks,))] * 2
@@ -574,9 +593,12 @@
         base = t * count
 
         def body(c, carry):
-            def mixed(lanes):
-                taps = [space_ref[k : k + 1, lanes] for k in range(9)]
-                times = [time_ref[k : k + 1, lanes] for k in range(TAPS)]
+            here = pl.ds(pl.multiple_of(c * LANES, LANES), LANES)
+
+            def mixed(kind):
+                lanes = pl.ds(pl.multiple_of(kind * chan + c * LANES, LANES), LANES)
+                taps = [space_ref[k, kind : kind + 1, here] for k in range(9)]
+                times = [time_ref[k, kind : kind + 1, here] for k in range(TAPS)]
 
                 def spatial(which, row):
                     loads = [
@@ -603,10 +625,10 @@
 
                 return over_time
 
-            value = mixed(pl.ds(pl.multiple_of(c * LANES, LANES), LANES))
-            gate = mixed(pl.ds(pl.multiple_of(chan + c * LANES, LANES), LANES))
+            value = mixed(0)
+            gate = mixed(1)
             for row in range(count):
-                gated[row * stride : (row + 1) * stride, pl.ds(pl.multiple_of(c * LANES, LANES), LANES)] = (
+                gated[row * stride : (row + 1) * stride, here] = (
                     value(row) * jax.nn.silu(gate(row))
                 ).astype(bf16)
             return carry
@@ -753,8 +775,8 @@
     )
 
     chan = w_inner.shape[2]
-    space = spatial_taps.reshape(9, 2 * chan)
-    time = temporal_taps.reshape(TAPS, 2 * chan)
+    space = spatial_taps.reshape((9,) + spatial_taps.shape[2:])
+    time = temporal_taps
     layer_out = finish(
         hidden, w_flat, w_down.T, space, time, tiles, blocks * pair, frames * col_count, col_count
     )

time: 171 us -> 161 us (0.942)
  Pallas kernels: 166 us -> 158 us
  local copies, waits for them, and re-layouts: 5.34 us -> 2.36 us
    pallas_call x1, Pallas kernels: 70.5 us -> 58.2 us  [front(): pl.pallas_call(functools.partial(front_kernel, (blocks, pair, ways, subs)...]
    pallas_call x1, Pallas kernels: 95.2 us -> 99.8 us  [finish(): pl.pallas_call(functools.partial(layer_kernel, (ways, halves, blks, strid...]
    unnamed x4 -> x1, local copies, waits for them, and re-layouts: 5.34 us -> 2.36 us
where the time goes in v3:
time: 161 us; the launch traced here: 160 us
  Pallas kernels  158 us (98%)
  local copies, waits for them, and re-layouts  2.36 us (1%)
    pallas_call x1, Pallas kernels, finish(): pl.pallas_call(functools.partial(layer_kernel, (ways, halves, blks, strid...  99.8 us
    pallas_call x1, Pallas kernels, front(): pl.pallas_call(functools.partial(front_kernel, (blocks, pair, ways, subs)...  58.2 us

profile of v3, /device:TPU:9, one launch (start us, length us, event | category | flops | bytes accessed | tf_op | source)
XLA Modules:
  0.0 160.4 jit_solution(16191515234627055017)
XLA Ops:
  0.0 58.2 %shard_map.91 = (bf16[256,2240]{1,0:T(8,128)(2,1)}, bf16[2240,2048]{1,0:T(8,128)(2,1)}) custom-call(bf16[256,2240]{1,0:T(8,128)(2,1)} %bitcast.9, bf16[256,2240]{1,0:T(8,128)(2,1)} %bitcast.10, bf16[256,2240]{1,0:T(8,128)(2,1)} %bitcast.11, bf16[256,2240]{1,0:T(8,128)(2,1)} %bitcast.12, bf16[560,2240]{1,0:T(8,128)(2,1)} %w_ref.1, ...), custom_call_target="tpu_custom_call" | custom-call | tf_op jit(solution)/shard_map/pallas_call | solution.py:327
  58.2 99.8 %shard_map.92 = bf16[256,2240]{1,0:T(8,128)(2,1)} custom-call(bf16[256,2240]{1,0:T(8,128)(2,1)} %get-tuple-element.7.hidden_ref, bf16[2240,2048]{1,0:T(8,128)(2,1)} %get-tuple-element.8.flat_ref, bf16[2240,1024]{1,0:T(8,128)(2,1)} %bitcast.8, f32[9,2,1024]{2,1,0:T(2,128)} %bitcast.13, f32[3,2,1024]{2,1,0:T(2,128)} %time_ref.1), custom_call_target="tpu_custom_call" | custom-call | tf_op jit(solution)/shard_map/pallas_call | solution.py:735
  158.0 2.4 %copy.11 = bf16[8,2,16,2240]{3,2,1,0:T(8,128)(2,1)} copy(bf16[8,2,16,2240]{3,2,1,0:T(8,128)(2,1)} %bitcast.7) | data formatting | bytes 2293760

commit v4 on v3

--- a/solution.py
+++ b/solution.py
@@ -88,8 +88,11 @@
     w_core = remote(w_ref, wbuf.at[tile], core_s.at[0], core_r.at[0], sibling)
     w_core.start()
 
+    def number_of(j, i):
+        return i * subs + j if j < subs else (i ^ 3) * subs + j - subs
+
     def y_send(s, j, i):
-        part = rows_of(i * subs + j, ids, rows)
+        part = rows_of(number_of(j, i), ids, rows)
         return remote(
             w_ref.at[part], wbuf.at[tile, part], ysend.at[s, j], yrecv.at[s, j],
             (blk, ((y + s) % ways) * 2 + core),
@@ -99,7 +102,7 @@
         return ((y + ways - s) % ways) * 2 + core
 
     def side_send(way, s, j, i):
-        part = rows_of(i * subs + j % subs, ids, rows)
+        part = rows_of(i * subs + j, ids, rows)
         place = wbuf.at[came(s), part]
         return remote(
             place, place, xsend.at[way, s, j], xrecv.at[way, s, j], across if way else beside
@@ -125,9 +128,10 @@
         def body(i):
             for s in range(1, ways):
                 y_send(s, j, i).wait_recv()
-                for way in range(2):
-                    side_send(way, s, j, i).start()
-                core_send(s, i * subs + j).start()
+                if j < subs:
+                    for way in range(2):
+                        side_send(way, s, j, i).start()
+                core_send(s, number_of(j, i)).start()
 
         each_quarter(body)
 
@@ -138,17 +142,7 @@
                 for way in range(2):
                     source = sources[way]
                     side_send(way, s, j, source).wait_recv()
-                    if way != j % 2:
-                        side_send(1 - way, s, subs + j, source).start()
                     core_send(s, source * subs + j).start()
-
-        each_quarter(body)
-
-    def relay_last(j):
-        def body(i):
-            for s in range(1, ways):
-                side_send(j % 2, s, subs + j, i ^ 3).wait_recv()
-                core_send(s, (i ^ 3) * subs + j).start()
 
         each_quarter(body)
 
@@ -201,6 +195,7 @@
         copy.start()
         first.append(copy)
     start_y(1)
+    relay_y(0)
     deinterleave(4, 8)
     total[...] = kv[core, rank].astype(jnp.float32) + got0[rank].astype(jnp.float32)
     for step in range(1, group):
@@ -219,10 +214,9 @@
         def _():
             later(step).start()
 
-    relay_y(0)
-    deinterleave(12, 10)
+    start_y(2)
+    deinterleave(12, 14)
     relay_y(1)
-    deinterleave(22, 4)
     relay_side(0)
 
     for step in range(1, blocks):
@@ -242,6 +236,7 @@
         third.append(copy)
     fourth = [remote(final_send, state.at[core, rank], send4.at[0], recv4.at[0], sibling)]
     fourth[0].start()
+    start_y(3)
     state[core, rank] = total[...].astype(jnp.bfloat16)
     deinterleave(26, steps - 26)
     flat_copy = pltpu.make_async_copy(flat, flat_ref, local.at[2])
@@ -252,7 +247,6 @@
         copy = remote(place, place, send4.at[step], recv4.at[step], sibling)
         copy.start()
         fourth.append(copy)
-    relay_side(1)
     for copy in fourth:
         copy.wait_recv()
 
@@ -264,8 +258,9 @@
         )
         ratio = both[:, :HEAD_DIM] / (both[:, HEAD_DIM : HEAD_DIM + 1] + EPS)
         attended[:, head_columns(head)] = ratio.astype(jnp.bfloat16)
-    relay_last(0)
-    relay_last(1)
+    relay_y(2)
+    relay_side(1)
+    relay_y(3)
     for t in range(2 * ways):
         pieces[t] = attended[:, t * rows : (t + 1) * rows]
 
@@ -297,13 +292,12 @@
             later(step).wait_send()
 
     def sent(i):
-        sources = (i ^ 2, i ^ 1)
         for s in range(1, ways):
+            for j in range(2 * subs):
+                y_send(s, j, i).wait_send()
             for j in range(subs):
-                y_send(s, j, i).wait_send()
                 for way in range(2):
                     side_send(way, s, j, i).wait_send()
-                side_send(j % 2, s, subs + j, sources[1 - j % 2]).wait_send()
 
     each_quarter(sent)
     for s in range(1, ways):
@@ -351,10 +345,10 @@
             dma((3,)),
             dma((2,)),
             dma((2,)),
-            dma((ways, subs)),
-            dma((ways, subs)),
-            dma((2, ways, 2 * subs)),
-            dma((2, ways, 2 * subs)),
+            dma((ways, 2 * subs)),
+            dma((ways, 2 * subs)),
+            dma((2, ways, subs)),
+            dma((2, ways, subs)),
             dma((ways, 4 * subs)),
             dma((ways, 4 * subs)),
         ]
@@ -463,12 +457,18 @@
             place, place, ysend.at[1, s, h], yrecv.at[1, s, h], (blk, there(s) * 2 + core)
         )
 
-    def to_core(s, t):
-        return remote(product.at[t], got.at[s], psend.at[s], precv.at[s], sibling)
-
-    def to_y(s):
+    def half_rows(ref, s, h):
+        return ref.at[s, pl.ds(h * part, part)]
+
+    def to_core(s, t, h):
         return remote(
-            sums.at[s], landed.at[s], rsend.at[s], rrecv.at[s], (blk, there(s) * 2 + core)
+            half_rows(product, t, h), half_rows(got, s, h), psend.at[s, h], precv.at[s, h], sibling
+        )
+
+    def to_y(s, h):
+        return remote(
+            half_rows(sums, s, h), half_rows(landed, s, h), rsend.at[s, h], rrecv.at[s, h],
+            (blk, there(s) * 2 + core),
         )
 
     has_next = blk + 1 < blks
@@ -589,8 +589,8 @@
     col = lax.broadcasted_iota(jnp.int32, (stride, LANES), 0) % cols
     masks = (col > 0, col < cols - 1)
 
-    def mix(t):
-        base = t * count
+    def mix(t, first, rows):
+        base = t * count + first
 
         def body(c, carry):
             here = pl.ds(pl.multiple_of(c * LANES, LANES), LANES)
@@ -627,7 +627,7 @@
 
             value = mixed(0)
             gate = mixed(1)
-            for row in range(count):
+            for row in range(rows):
                 gated[row * stride : (row + 1) * stride, here] = (
                     value(row) * jax.nn.silu(gate(row))
                 ).astype(bf16)
@@ -635,13 +635,17 @@
 
         lax.fori_loop(0, chan // LANES, body, 0)
         result = lax.dot_general(
-            gated[...], down[...], (((1,), (1,)), ((), ())), preferred_element_type=f32
-        )
-        product[t] = result.astype(bf16)
+            gated[: rows * stride], down[...], (((1,), (1,)), ((), ())), preferred_element_type=f32
+        )
+        product[t, first * stride : (first + rows) * stride] = result.astype(bf16)
 
     def own_rows(t):
-        mix(t)
-        pl.when(core != t % 2)(to_core(0, t).start)
+        mix(t, 0, count)
+
+        @pl.when(core != t % 2)
+        def _():
+            for h in every:
+                to_core(0, t, h).start()
 
     down_copy.wait()
     early = [y * (tiles - 1)] if ways == 2 else []
@@ -674,26 +678,31 @@
     for s in others:
         for c in range(2):
             t = there(s) * 2 + c
-            mix(t)
-            pl.when(core != c)(to_core(s, t).start)
-
-            @pl.when(core == c)
-            def _():
-                to_core(s, t).wait_recv()
-                sums[s] = (product[t].astype(f32) + got[s].astype(f32)).astype(bf16)
-                to_y(s).start()
+            for h in every:
+                mix(t, h * part // stride, part // stride)
+                pl.when(core != c)(to_core(s, t, h).start)
+
+                @pl.when(core == c)
+                def _():
+                    to_core(s, t, h).wait_recv()
+                    where = slice(h * part, (h + 1) * part)
+                    sums[s, where] = (
+                        product[t, where].astype(f32) + got[s, where].astype(f32)
+                    ).astype(bf16)
+                    to_y(s, h).start()
 
     for t in late:
         own_rows(t)
-    to_core(0, tile).wait_recv()
-    for s in others:
-        to_y(s).wait_recv()
-    for start in range(0, tokens, stride):
-        where = slice(start, start + stride)
-        total = product[tile, where].astype(f32) + got[0, where].astype(f32)
+    for h in every:
+        to_core(0, tile, h).wait_recv()
         for s in others:
-            total = total + landed[s, where].astype(f32)
-        out_ref[where] = (hidden_ref[where].astype(f32) + total).astype(bf16)
+            to_y(s, h).wait_recv()
+        for start in range(h * part, (h + 1) * part, stride):
+            where = slice(start, start + stride)
+            total = product[tile, where].astype(f32) + got[0, where].astype(f32)
+            for s in others:
+                total = total + landed[s, where].astype(f32)
+            out_ref[where] = (hidden_ref[where].astype(f32) + total).astype(bf16)
 
     for h in every:
         own_core(h).wait_send()
@@ -716,10 +725,11 @@
                 for s in others:
                     before_y(s, h).wait_send()
 
-    for s in range(ways):
-        to_core(s, tile).wait_send()
-    for s in others:
-        to_y(s).wait_send()
+    for h in every:
+        for s in range(ways):
+            to_core(s, tile, h).wait_send()
+        for s in others:
+            to_y(s, h).wait_send()
 
 
 def finish(hidden, flat, down, space, time, tiles, blks, stride, cols):
@@ -750,8 +760,7 @@
             dma((1 + 2 * chan // FILL,)),
         ]
         + [dma((2, ways, halves))] * 4
-        + [dma((ways, halves))] * 2
-        + [dma((ways,))] * 4,
+        + [dma((ways, halves))] * 6,
         compiler_params=pltpu.CompilerParams(
             collective_id=1, has_side_effects=True, vmem_limit_bytes=61 * 2**20
         ),

time: 161 us -> 147 us (0.913)
  Pallas kernels: 158 us -> 144 us
    pallas_call x1, Pallas kernels: 58.2 us -> 51.2 us  [front(): pl.pallas_call(functools.partial(front_kernel, (blocks, pair, ways, subs)...]
    pallas_call x1, Pallas kernels: 99.8 us -> 92.9 us  [finish(): pl.pallas_call(functools.partial(layer_kernel, (ways, halves, blks, strid...]
where the time goes in v4:
time: 147 us
  Pallas kernels  144 us (98%)
  local copies, waits for them, and re-layouts  2.36 us (2%)
    pallas_call x1, Pallas kernels, finish(): pl.pallas_call(functools.partial(layer_kernel, (ways, halves, blks, strid...  92.9 us
    pallas_call x1, Pallas kernels, front(): pl.pallas_call(functools.partial(front_kernel, (blocks, pair, ways, subs)...  51.2 us

profile of v4, /device:TPU:9, one launch (start us, length us, event | category | flops | bytes accessed | tf_op | source)
XLA Modules:
  0.0 146.5 jit_solution(18232023729016705107)
XLA Ops:
  0.0 51.2 %shard_map.91 = (bf16[256,2240]{1,0:T(8,128)(2,1)}, bf16[2240,2048]{1,0:T(8,128)(2,1)}) custom-call(bf16[256,2240]{1,0:T(8,128)(2,1)} %bitcast.9, bf16[256,2240]{1,0:T(8,128)(2,1)} %bitcast.10, bf16[256,2240]{1,0:T(8,128)(2,1)} %bitcast.11, bf16[256,2240]{1,0:T(8,128)(2,1)} %bitcast.12, bf16[560,2240]{1,0:T(8,128)(2,1)} %w_ref.1, ...), custom_call_target="tpu_custom_call" | custom-call | tf_op jit(solution)/shard_map/pallas_call | solution.py:321
  51.2 92.9 %shard_map.92 = bf16[256,2240]{1,0:T(8,128)(2,1)} custom-call(bf16[256,2240]{1,0:T(8,128)(2,1)} %get-tuple-element.7.hidden_ref, bf16[2240,2048]{1,0:T(8,128)(2,1)} %get-tuple-element.8.flat_ref, bf16[2240,1024]{1,0:T(8,128)(2,1)} %bitcast.8, f32[9,2,1024]{2,1,0:T(2,128)} %bitcast.13, f32[3,2,1024]{2,1,0:T(2,128)} %time_ref.1), custom_call_target="tpu_custom_call" | custom-call | tf_op jit(solution)/shard_map/pallas_call | solution.py:745
  144.1 2.4 %copy.11 = bf16[8,2,16,2240]{3,2,1,0:T(8,128)(2,1)} copy(bf16[8,2,16,2240]{3,2,1,0:T(8,128)(2,1)} %bitcast.7) | data formatting | bytes 2293760
